TPU v7x, 128 devices: a whole 4x4x4 slice. The times are simulated.
128 devices in a mesh: ctx: 32 (over x, y, core), heads: 4 (over z).
Axes of the slice: x: 4, y: 4, z: 4, core: 2. Of those that a mesh axis runs over, the one named last changes fastest.
Arguments:
- queries: bfloat16 [32, 32768, 128], P('heads', 'ctx'), may hold values from -6 to 6
- keys: bfloat16 [32, 32768, 128], P('heads', 'ctx'), may hold values from -6 to 6
- values: bfloat16 [32, 32768, 128], P('heads', 'ctx'), may hold values from -6 to 6
- out_grad: bfloat16 [32, 32768, 128], P('heads', 'ctx'), may hold values from -6 to 6
- level_table: float32 [64, 16], replicated, may hold values from 0.2 to 2
- table_index: int32 [32768], P('ctx'), may hold values from 0 to 63
Outputs:
- attention_out: bfloat16 [32, 32768, 128], P('heads', 'ctx')
- query_grad: bfloat16 [32, 32768, 128], P('heads', 'ctx')
- key_grad: bfloat16 [32, 32768, 128], P('heads', 'ctx')
- value_grad: bfloat16 [32, 32768, 128], P('heads', 'ctx')
- table_grad: float32 [64, 16], replicated
All inputs are finite; a program needn't handle non-finite values.
Results may differ from a plain program's by a relative error of at most 0.0058.
Values sent between devices are 32-bit elements; how exact they have to be, the bound alone decides.
A program may use at most 256 MiB of HBM per device.

v0:
```python
import math

import jax
import jax.numpy as jnp
from jax import lax
from jax.sharding import PartitionSpec as P


def level_grid(length):
    row_ids = lax.broadcasted_iota(jnp.int32, (length, length), 0)
    col_ids = lax.broadcasted_iota(jnp.int32, (length, length), 1)
    crossed = jnp.bitwise_xor(row_ids, col_ids)
    levels = jnp.zeros((length, length), jnp.int32)
    for bit_pos in range(length.bit_length()):
        levels = levels + (crossed >= 1 << bit_pos).astype(jnp.int32)
    return (levels, col_ids <= row_ids)


def lookup(level_table, table_index):
    matches = table_index[:, None] == jnp.arange(level_table.shape[0], dtype=jnp.int32)[None, :]
    lam_all = jnp.sum(jnp.where(matches[:, :, None], level_table[None], 0.0), 1)
    return (matches, lam_all)


def block_start(queries, keys, values, out_grad, lam_tok, block_id, level_bits, factor):
    first_cross = queries.shape[1].bit_length()
    states = jnp.einsum("htd,hte->hde", keys, values, preferred_element_type=jnp.float32)
    pieces = []
    for bit_num in range(level_bits):
        scaled = (lam_tok[:, first_cross + bit_num][None, :, None] * out_grad).astype(jnp.bfloat16)
        upper_half = jnp.right_shift(block_id, bit_num) & 1 == 1
        bucket_grad = factor * jnp.einsum(
            "htd,hte->hde", queries, scaled, preferred_element_type=jnp.float32
        )
        pieces.append(jnp.where(upper_half, bucket_grad, jnp.zeros_like(bucket_grad)))
    return (states, jnp.stack(pieces))


def block_finish(queries, keys, values, out_grad, lam_tok, bucket, state_grad, factor):
    length = queries.shape[1]
    level_bits = bucket.shape[0]
    first_cross = length.bit_length()
    levels, causal = level_grid(length)
    weight = jnp.zeros((length, length), jnp.float32)
    for level_id in range(first_cross):
        weight = weight + jnp.where(levels == level_id, lam_tok[:, level_id : level_id + 1], 0.0)
    weight = factor * jnp.where(causal, weight, 0.0)
    dot_scores = jnp.einsum("htd,hsd->hts", queries, keys, preferred_element_type=jnp.float32)
    weighted = (weight[None] * dot_scores).astype(jnp.bfloat16)
    out_local = jnp.einsum("hts,hsd->htd", weighted, values, preferred_element_type=jnp.float32)
    grad_weighted = jnp.einsum("htd,hsd->hts", out_grad, values, preferred_element_type=jnp.float32)
    grad_scores = (weight[None] * grad_weighted).astype(jnp.bfloat16)
    query_local = jnp.einsum("hts,hsd->htd", grad_scores, keys, preferred_element_type=jnp.float32)
    key_local = jnp.einsum("hts,htd->hsd", grad_scores, queries, preferred_element_type=jnp.float32)
    value_local = jnp.einsum("hts,htd->hsd", weighted, out_grad, preferred_element_type=jnp.float32)
    weight_grad = jnp.sum(dot_scores * grad_weighted, 0)
    lam_cross = lam_tok[:, first_cross : first_cross + level_bits].T[:, None, :, None]
    cross = jnp.einsum("htd,jhde->jhte", queries, bucket, preferred_element_type=jnp.float32)
    attention_out = out_local + factor * jnp.sum(lam_cross * cross, 0)
    back_cross = jnp.einsum("hte,jhde->jhtd", out_grad, bucket, preferred_element_type=jnp.float32)
    query_grad = query_local + factor * jnp.sum(lam_cross * back_cross, 0)
    key_grad = key_local + jnp.einsum(
        "hte,hde->htd", values, state_grad, preferred_element_type=jnp.float32
    )
    value_grad = value_local + jnp.einsum(
        "htd,hde->hte", keys, state_grad, preferred_element_type=jnp.float32
    )
    local_cols = [
        factor * jnp.sum(jnp.where(causal & (levels == level_id), weight_grad, 0.0), 1)
        for level_id in range(first_cross)
    ]
    lam_local = jnp.stack(local_cols, 1)
    lam_far = factor * jnp.sum(cross * out_grad.astype(jnp.float32)[None], axis=(1, 3))
    spare = jnp.zeros((length, lam_tok.shape[1] - first_cross - level_bits), jnp.float32)
    lam_grad = jnp.concatenate([lam_local, lam_far.T, spare], 1)
    return (
        attention_out.astype(jnp.bfloat16),
        query_grad.astype(jnp.bfloat16),
        key_grad.astype(jnp.bfloat16),
        value_grad.astype(jnp.bfloat16),
        lam_grad,
    )


def in_bucket(owners, block_id, bit_num):
    same_top = jnp.right_shift(owners, bit_num + 1) == jnp.right_shift(block_id, bit_num + 1)
    owner_low = jnp.right_shift(owners, bit_num) & 1 == 0
    mine_high = jnp.right_shift(block_id, bit_num) & 1 == 1
    return same_top & owner_low & mine_high


def body(queries, keys, values, out_grad, level_table, table_index):
    head_local, length, head_width = queries.shape
    devices = lax.axis_size("ctx")
    level_bits = devices.bit_length() - 1
    factor = 1.0 / math.sqrt(head_width * length * devices)
    block_id = lax.axis_index("ctx")
    matches, lam_tok = lookup(level_table, table_index)
    states, grads = block_start(
        queries, keys, values, out_grad, lam_tok, block_id, level_bits, factor
    )
    shard_piece = lax.all_gather(states[None], "ctx", axis=0, tiled=True)
    owners = jnp.arange(shard_piece.shape[0], dtype=jnp.int32)
    pieces = []
    for bit_num in range(level_bits):
        member = in_bucket(owners, block_id, bit_num)
        pieces.append(jnp.sum(jnp.where(member[:, None, None, None], shard_piece, 0.0), 0))
    bucket = jnp.stack(pieces)
    bucket = bucket.astype(jnp.bfloat16)
    row_total = head_local * lax.axis_size("ctx")
    owners = jnp.arange(row_total // head_local, dtype=jnp.int32)
    term = jnp.zeros((row_total // head_local,) + states.shape, jnp.float32)
    for bit_num in range(level_bits):
        member = in_bucket(owners, block_id, bit_num)
        term = term + jnp.where(member[:, None, None, None], grads[bit_num][None], 0.0)
    state_grad = lax.psum_scatter(
        term.reshape((row_total,) + states.shape[1:]), "ctx", scatter_dimension=0, tiled=True
    )
    state_grad = state_grad.astype(jnp.bfloat16)
    attention_out, query_grad, key_grad, value_grad, lam_grad = block_finish(
        queries, keys, values, out_grad, lam_tok, bucket, state_grad, factor
    )
    table_part = jnp.sum(jnp.where(matches[:, :, None], lam_grad[:, None, :], 0.0), 0)
    table_total = lax.psum(table_part, ("ctx", "heads"))
    table_grad = table_total / math.sqrt(length * devices)
    return (attention_out, query_grad, key_grad, value_grad, table_grad)


def solution(mesh):
    placed = (
        P("heads", "ctx", None),
        P("heads", "ctx", None),
        P("heads", "ctx", None),
        P("heads", "ctx", None),
        P(),
        P("ctx"),
    )
    return jax.shard_map(
        body,
        mesh=mesh,
        in_specs=placed,
        out_specs=(
            P("heads", "ctx", None),
            P("heads", "ctx", None),
            P("heads", "ctx", None),
            P("heads", "ctx", None),
            P(),
        ),
        check_vma=False,
    )
```

profile of v0, /device:TPU:1, one launch (start us, length us, event | category | flops | bytes accessed | tf_op | source)
XLA Modules:
  0.0 370.0 jit_solution(8418169630844257545)
XLA Ops:
  7.3 0.1 broadcast_in_dim.340
  7.3 0.1 broadcast_in_dim.341
  7.4 0.1 broadcast_in_dim.335
  7.5 0.1 broadcast_in_dim.336
  7.6 0.1 broadcast_in_dim.350
  7.7 0.1 broadcast_in_dim.351
  7.9 0.1 broadcast_in_dim.346
  8.1 0.1 broadcast_in_dim.330
  8.2 0.8 copy.72
  9.0 0.9 iota_compare_fusion.1
  9.9 0.6 copy-done.7
  10.5 0.5 select_reduce_fusion.17
  11.1 2.6 fusion.100
  13.7 1.1 fusion.64
  14.9 1.1 fusion.91
  16.0 1.1 fusion.82
  17.1 1.1 fusion.73
  18.3 8.7 %fusion.2 = f32[256,128,128]{1,2,0:T(8,128)} fusion(f32[8,128,128]{1,2,0:T(8,128)S(1)} %fusion.100, f32[8,128,128]{1,2,0:T(8,128)S(1)} %fusion.91, f32[8,128,128]{1,2,0:T(8,128)S(1)} %fusion.82, f32[8,128,128]{1,2,0:T(8,128)S(1)} %fusion.73, f32[8,128,128]{1,2,0:T(8,128)S(1)} %fusion.64, pred[256]{0:T(512)(128)(4,1)S(1)} %broadcast_in_dim.351, ...), kind=kLoop, calls=%fused_computation.9 | loop fusion | flops 37748736 | bytes 19399936 | tf_op jit(solution)/shard_map/add | solution.py:115
  27.0 0.2 all-gather.3.cloned.1.call-start
  27.2 3.8 %fusion.106 = f32[8,128,128]{2,1,0:T(8,128)} fusion(bf16[8,1024,128]{2,1,0:T(8,128)(2,1)} %param.7, bf16[8,1024,128]{2,1,0:T(8,128)(2,1)} %param.8), kind=kOutput, calls=%fused_computation.153 | convolution fusion | flops 268435456 | bytes 4718592 | tf_op jit(solution)/shard_map/htd,hte->hde/dot_general | solution.py:27
  31.1 4.1 %copy.92 = f32[8,1024,128]{1,2,0:T(8,128)} copy(bf16[8,1024,128]{2,1,0:T(8,128)(2,1)} %param.9) | data formatting | bytes 6291456 | tf_op jit(solution)/shard_map/convert_element_type | solution.py:30
  35.2 21.5 %fusion.107 = f32[8,1024,1024]{2,1,0:T(8,128)} fusion(bf16[8,1024,128]{2,1,0:T(8,128)(2,1)} %param.9, bf16[8,1024,128]{2,1,0:T(8,128)(2,1)} %param.8), kind=kOutput, calls=%fused_computation.154 | convolution fusion | flops 2147483648 | bytes 37748736 | tf_op jit(solution)/shard_map/htd,hsd->hts/dot_general | solution.py:51
  56.7 30.6 %multiply_reduce_fusion = (f32[1024,1024]{1,0:T(8,128)}, f32[8,1024,1024]{2,1,0:T(8,128)}) fusion(f32[8,1024,1024]{2,1,0:T(8,128)} %fusion.107, bf16[8,1024,128]{2,1,0:T(8,128)(2,1)S(1)} %copy-done, bf16[8,1024,128]{2,1,0:T(8,128)(2,1)} %param.7), kind=kOutput, calls=%fused_computation | convolution fusion | flops 2163212288 | bytes 75497472 | tf_op jit(solution)/shard_map/htd,hsd->hts/dot_general | solution.py:48
  87.3 18.2 %select_reduce_fusion.6 = (f32[1024]{0:T(1024)S(1)}, f32[1024]{0:T(1024)S(1)}, f32[1024]{0:T(1024)S(1)}, f32[1024]{0:T(1024)S(1)}, f32[1024]{0:T(1024)S(1)}, /*i...) fusion(f32[1024,1024]{1,0:T(8,128)} %get-tuple-element.44), kind=kLoop, calls=%fused_computation.43 | loop fusion | flops 81777664 | bytes 4239360 | tf_op jit(solution)/shard_map/reduce_sum | solution.py:69
  105.6 9.6 %select_multiply_fusion = f32[1024,1024]{1,0:T(8,128)S(1)} fusion(f32[1024]{0:T(1024)S(1)} %bitcast.129, f32[1024]{0:T(1024)S(1)} %bitcast.130, f32[1024]{0:T(1024)S(1)} %bitcast.131, f32[1024]{0:T(1024)S(1)} %bitcast.132, f32[1024]{0:T(1024)S(1)} %bitcast.133, f32[1024]{0:T(1024)S(1)} %bitcast.134, f32[1024]{0:T(1024)S(1)} %bitcast.135, ...), kind=kLoop, calls=%fused_computation.55 | loop fusion | flops 71303168 | bytes 4239360 | tf_op jit(solution)/shard_map/mul | solution.py:47
  115.2 18.0 %fusion.8 = f32[8,1024,128]{2,1,0:T(8,128)} fusion(bf16[8,1024,128]{2,1,0:T(8,128)(2,1)S(1)} %copy-done, f32[8,1024,1024]{2,1,0:T(8,128)} %fusion.107, f32[1024,1024]{1,0:T(8,128)S(1)} %select_multiply_fusion), kind=kOutput, calls=%fused_computation.29 | convolution fusion | flops 2164260864 | bytes 44040192 | tf_op jit(solution)/shard_map/hts,htd->hsd/dot_general | solution.py:54
  133.2 17.5 %fusion.6 = f32[8,1024,128]{2,1,0:T(8,128)} fusion(bf16[8,1024,128]{2,1,0:T(8,128)(2,1)} %param.9, f32[8,1024,1024]{2,1,0:T(8,128)} %get-tuple-element.45, f32[1024,1024]{1,0:T(8,128)S(1)} %select_multiply_fusion), kind=kOutput, calls=%fused_computation.27 | convolution fusion | flops 2164260864 | bytes 44040192 | tf_op jit(solution)/shard_map/hts,htd->hsd/dot_general | solution.py:55
  150.8 5.1 %fusion.16 = bf16[8,1024,128]{2,1,0:T(8,128)(2,1)} fusion(f32[8,1024,128]{2,1,0:T(8,128)} %fusion.8, bf16[8,1024,128]{2,1,0:T(8,128)(2,1)} %param.8, f32[8,128,128]{1,2,0:T(8,128)} %reduce-scatter.2.cloned.1.call-done), kind=kOutput, calls=%fused_computation.39 | convolution fusion | flops 270663680 | bytes 8912896 | tf_op jit(solution)/shard_map/hte,hde->htd/dot_general | solution.py:62
  155.9 2.0 fusion.15
  158.0 62.7 %all-gather.3.cloned.1.call-done = f32[256,128,128]{2,1,0:T(8,128)} async-done(((f32[8,128,128]{2,1,0:T(8,128)}), f32[256,128,128]{2,1,0:T(8,128)}) %all-gather.3.cloned.1.call-update) | async-done | bytes 16777232 | tf_op jit(solution)/shard_map/all_gather | solution.py:102
  220.7 12.3 %select_reduce_fusion = (bf16[8,128,128]{2,1,0:T(8,128)(2,1)S(1)}, bf16[8,128,128]{2,1,0:T(8,128)(2,1)S(1)}, bf16[8,128,128]{2,1,0:T(8,128)(2,1)S(1)}, bf16[8,12...) fusion(f32[32,8,128,128]{3,2,1,0:T(8,128)} %bitcast.128, pred[32]{0:T(512)(128)(4,1)S(1)} %get-tuple-element.46, ...), kind=kLoop, calls=%fused_computation.17 | loop fusion | flops 41287680 | bytes 18088096 | tf_op jit(solution)/shard_map/reduce_sum | solution.py:107
  233.0 0.9 copy.78
  233.9 0.8 copy.77
  234.7 0.2 copy.76
  234.9 0.2 copy.75
  235.1 0.2 copy.74
  235.4 1.0 bitcast_dynamic-update-slice_fusion.1
  236.5 1.0 copy-done.9
  237.5 6.8 %multiply_reduce_fusion.1 = f32[8,128,1024]{2,1,0:T(8,128)} fusion(f32[5,1024]{1,0:T(8,128)S(1)} %slice_bitcast_fusion, bf16[5,8,128,128]{2,3,0,1:T(8,128)(2,1)S(1)} %bitcast_dynamic-update-slice_fusion, bf16[8,1024,128]{2,1,0:T(8,128)(2,1)} %param.9), kind=kOutput, calls=%fused_computation.7 | convolution fusion | flops 1351614464 | bytes 7622656 | tf_op jit(solution)/shard_map/hte,jhde->jhtd/dot_general | solution.py:60
  244.3 5.4 %copy.81 = f32[8,128,1024]{1,2,0:T(8,128)} copy(f32[8,128,1024]{2,1,0:T(8,128)} %multiply_reduce_fusion.1) | data formatting | bytes 8388608 | tf_op jit(solution)/shard_map/reduce_sum | solution.py:61
  249.7 7.2 %fusion.1 = (f32[5,1024]{1,0:T(8,128)S(1)}, f32[8,1024,128]{1,2,0:T(8,128)}) fusion(f32[8,1024,128]{1,2,0:T(8,128)} %copy.92, f32[5,1024]{1,0:T(8,128)S(1)} %slice_bitcast_fusion, bf16[5,8,128,128]{2,3,0,1:T(8,128)(2,1)S(1)} %copy-done.10, bf16[8,1024,128]{2,1,0:T(8,128)(2,1)S(1)} %copy-done), kind=kOutput, calls=%fused_computation.6 | convolution fusion | flops 1362095104 | bytes 11837440 | tf_op jit(solution)/shard_map/htd,jhde->jhte/dot_general | solution.py:58
  256.9 5.3 %copy.79 = f32[8,1024,128]{2,1,0:T(8,128)} copy(f32[8,1024,128]{1,2,0:T(8,128)} %get-tuple-element.11) | data formatting | bytes 8388608 | tf_op jit(solution)/shard_map/reduce_sum | solution.py:59
  262.2 17.4 %fusion.17 = bf16[8,1024,128]{2,1,0:T(8,128)(2,1)} fusion(f32[8,128,1024]{1,2,0:T(8,128)} %copy.81, bf16[8,1024,128]{2,1,0:T(8,128)(2,1)} %param.7, f32[8,1024,1024]{2,1,0:T(8,128)} %fusion.107, f32[1024,1024]{1,0:T(8,128)} %copy-done.1), kind=kOutput, calls=%fused_computation.41 | convolution fusion | flops 2167406592 | bytes 46137344 | tf_op jit(solution)/shard_map/hts,hsd->htd/dot_general | solution.py:53
  279.7 17.3 %add_convert_fusion = bf16[8,1024,128]{2,1,0:T(8,128)(2,1)} fusion(f32[8,1024,128]{2,1,0:T(8,128)} %copy.79, bf16[8,1024,128]{2,1,0:T(8,128)(2,1)} %param.8, f32[8,1024,1024]{2,1,0:T(8,128)} %get-tuple-element.45, f32[1024,1024]{1,0:T(8,128)} %copy-done.1), kind=kOutput, calls=%fused_computation.54 | convolution fusion | flops 2167406592 | bytes 46137344 | tf_op jit(solution)/shard_map/hts,hsd->htd/dot_general | solution.py:50
  296.9 0.1 concatenate.3
  297.0 0.5 select_reduce_fusion.5
  297.5 64.7 %psum.7 = f32[64,16]{1,0:T(8,128)S(1)} all-reduce(f32[64,16]{1,0:T(8,128)S(1)} %select_reduce_fusion.5), channel_id=1, replica_groups=mesh['ctx'=32,'heads'=4] {'ctx','heads'}, use_global_device_ids=true, to_apply=%region_23.24 | all-reduce | flops 1024 | bytes 8192 | tf_op jit(solution)/shard_map/psum | solution.py:124
  362.3 0.7 copy.93
  (43 shorter events, 0.5 us)
Async XLA Ops:
  7.2 3.9 %copy-start = (bf16[8,1024,128]{2,1,0:T(8,128)(2,1)S(1)}, bf16[8,1024,128]{2,1,0:T(8,128)(2,1)}, u32[]{:S(2)}) copy-start(bf16[8,1024,128]{2,1,0:T(8,128)(2,1)} %param.6) | copy-start | bytes 6291460
  7.2 143.6 %reduce-scatter.2.cloned.1.call-start = ((), (), s32[]{:S(2)}) async-start(), calls=%async_computation.1 | async-start | bytes 17301504 | tf_op jit(solution)/shard_map/reduce_scatter | solution.py:116
  9.0 4.8 %copy-start.3 = (bf16[8,1024,128]{2,1,0:T(8,128)(2,1)S(1)}, bf16[8,1024,128]{2,1,0:T(8,128)(2,1)}, u32[]{:S(2)}) copy-start(bf16[8,1024,128]{2,1,0:T(8,128)(2,1)} %param.9) | copy-start | bytes 6291460
  9.8 0.6 copy-start.7
  27.0 193.7 %all-gather.3.cloned.1.call-start = ((), (), s32[]{:S(2)}) async-start(), calls=%async_computation.2 | async-start | bytes 17301504 | tf_op jit(solution)/shard_map/all_gather | solution.py:102
  115.2 18.0 %copy-start.1 = (f32[1024,1024]{1,0:T(8,128)}, f32[1024,1024]{1,0:T(8,128)S(1)}, u32[]{:S(2)}) copy-start(f32[1024,1024]{1,0:T(8,128)S(1)} %select_multiply_fusion) | copy-start | bytes 12582916
  150.8 5.2 %copy-start.2 = (bf16[8,1024,128]{2,1,0:T(8,128)(2,1)S(1)}, bf16[8,1024,128]{2,1,0:T(8,128)(2,1)}, u32[]{:S(2)}) copy-start(bf16[8,1024,128]{2,1,0:T(8,128)(2,1)} %param.7) | copy-start | bytes 6291460
  150.8 5.2 %copy-start.4 = (f32[8,1024,128]{2,1,0:T(8,128)S(1)}, f32[8,1024,128]{2,1,0:T(8,128)}, u32[]{:S(2)}) copy-start(f32[8,1024,128]{2,1,0:T(8,128)} %fusion.6) | copy-start | bytes 12582916
  150.8 5.2 %copy-start.5 = (f32[8,128,128]{1,2,0:T(8,128)S(1)}, f32[8,128,128]{1,2,0:T(8,128)}, u32[]{:S(2)}) copy-start(f32[8,128,128]{1,2,0:T(8,128)} %reduce-scatter.2.cloned.1.call-done) | copy-start | bytes 1572868
  233.9 2.5 copy-start.6
  236.5 1.1 copy-start.9
  244.3 5.4 %copy-start.10 = (bf16[5,8,128,128]{2,3,0,1:T(8,128)(2,1)S(1)}, bf16[5,8,128,128]{2,3,0,1:T(8,128)(2,1)}, u32[]{:S(2)}) copy-start(bf16[5,8,128,128]{2,3,0,1:T(8,128)(2,1)} %copy-done.9) | copy-start | bytes 3932164
  279.7 17.4 %copy-start.8 = (pred[1024,64]{0,1:T(8,128)(4,1)S(1)}, pred[1024,64]{0,1:T(8,128)(4,1)}, u32[]{:S(2)}) copy-start(pred[1024,64]{0,1:T(8,128)(4,1)} %copy-done.7) | copy-start | bytes 196612
Sparse Core Ops, SparseCore 0:
  27.1 117.0 reduce-scatter.1
  147.1 73.5 all-gather.2
where the time goes:
time: 376 us; the launch traced here: 370 us
  matrix products  154 us (41%)
  blocking collectives  64.7 us (17%)
  waiting for transfers between devices  62.8 us (17%)
  other arithmetic  50.8 us (14%)
  local copies, waits for them, and re-layouts  22.4 us (6%)
  between operations  14.6 us (4%)
    psum x1, blocking collectives, body(): table_total = lax.psum(table_part, ('ctx', 'heads'))  64.7 us
    all_gather x1, waiting for transfers between devices, body(): shard_piece = lax.all_gather(states[None], 'ctx', axis=0, tiled=True)  62.7 us
    dot_general x1, matrix products, block_finish(): jnp.einsum('htd,hsd->hts', queries, keys, preferred_element_type=jnp.floa...  30.6 us
    dot_general x1, matrix products, block_finish(): jnp.einsum('htd,hsd->hts', out_grad, values, preferred_element_type=jnp.f...  21.5 us
    reduce_sum x1, other arithmetic, block_finish(): jnp.sum(jnp.where(causal & (levels == level_id), weight_grad, 0.0), 1)  18.2 us
    dot_general x1, matrix products, block_finish(): jnp.einsum('hts,htd->hsd', grad_scores, queries, preferred_element_type=j...  18 us
    dot_general x1, matrix products, block_finish(): jnp.einsum('hts,htd->hsd', weighted, out_grad, preferred_element_type=jnp...  17.5 us
    dot_general x1, matrix products, block_finish(): jnp.einsum('hts,hsd->htd', grad_scores, keys, preferred_element_type=jnp....  17.4 us
  transfers between devices with their start and end apart: 2, of which 1 were waited for; matrix products, arithmetic and copies ran while one was open for 35% of the time, Pallas kernels for 0%

commit v1 on v0

v1 whole, which is shorter than its diff:
```python
import functools
import math

import jax
import jax.numpy as jnp
from jax import lax
from jax.experimental import pallas as pl
from jax.experimental.pallas import tpu as pltpu
from jax.sharding import PartitionSpec as P

SUB = 256
F32 = jnp.float32
BF16 = jnp.bfloat16
NN = (((1,), (0,)), ((), ()))
NT = (((1,), (1,)), ((), ()))
TN = (((0,), (0,)), ((), ()))


def mm(a, b, dims):
    return lax.dot_general(a, b, dims, preferred_element_type=F32)


def split3(value):
    first = value.astype(BF16)
    rest = value - first.astype(F32)
    second = rest.astype(BF16)
    third = (rest - second.astype(F32)).astype(BF16)
    return first, second, third


def one_hot(index_row, rows):
    length = index_row.shape[1]
    row_ids = lax.broadcasted_iota(jnp.int32, (rows, length), 0)
    return jnp.where(row_ids == index_row, 1.0, 0.0).astype(BF16)


def fill_lambda(index_ref, table_ref, wide_ref, diag_ref, factor):
    hot = one_hot(index_ref[...], table_ref.shape[0])
    parts = split3(table_ref[...] * factor)
    lam = sum(mm(hot, part, TN) for part in parts)
    length = lam.shape[0]
    for level in range(wide_ref.shape[0]):
        column = lam[:, 9 + level : 10 + level]
        wide_ref[level] = jnp.broadcast_to(column, (length, 128))
    rows = lax.broadcasted_iota(jnp.int32, (SUB, SUB), 0)
    cols = lax.broadcasted_iota(jnp.int32, (SUB, SUB), 1)
    crossed = jnp.bitwise_xor(rows, cols)
    for tile in range(length // SUB):
        part = lam[tile * SUB : (tile + 1) * SUB]
        weight = jnp.broadcast_to(part[:, 0:1], (SUB, SUB))
        for level in range(1, 9):
            weight = jnp.where(crossed >= 1 << (level - 1), part[:, level : level + 1], weight)
        diag_ref[tile] = jnp.where(cols <= rows, weight, 0.0)


def pre_kernel(q_ref, k_ref, v_ref, g_ref, index_ref, table_ref, state_ref, grad_ref, wide, diag, *, factor):
    head = pl.program_id(0)

    @pl.when(head == 0)
    def _():
        fill_lambda(index_ref, table_ref, wide, diag, factor)

    state_ref[0] = mm(k_ref[0], v_ref[0], TN)
    grad = g_ref[0].astype(F32)
    block_id = lax.axis_index("ctx")
    scaled = jnp.concatenate([(wide[2 + j] * grad).astype(BF16) for j in range(5)], axis=1)
    total = mm(q_ref[0], scaled, TN)
    for j in range(5):
        keep = (block_id >> j) & 1 == 1
        grad_ref[j, 0] = jnp.where(keep, total[:, j * 128 : (j + 1) * 128], 0.0)


def main_kernel(
    q_ref, k_ref, v_ref, g_ref, index_ref, table_ref, bucket_ref, sgrad_ref,
    out_ref, qg_ref, kg_ref, vg_ref, part_ref,
    wide, diag, wsum, lsum, *, factor,
):
    head = pl.program_id(0)

    @pl.when(head == 0)
    def _():
        fill_lambda(index_ref, table_ref, wide, diag, factor)
        wsum[...] = jnp.zeros_like(wsum)
        lsum[...] = jnp.zeros_like(lsum)

    tiles = q_ref.shape[1] // SUB
    states = [mm(k_ref[0, pl.ds(c * SUB, SUB)], v_ref[0, pl.ds(c * SUB, SUB)], TN) for c in range(3)]
    near = {1: states[0].astype(BF16), 3: states[2].astype(BF16)}
    pair = (states[0] + states[1]).astype(BF16)
    far_bucket = bucket_ref[0].astype(BF16)
    far_grad = sgrad_ref[0]
    near_grad = {}
    pair_grad = None
    for c in range(tiles):
        rows = pl.ds(c * SUB, SUB)
        q, grad = q_ref[0, rows], g_ref[0, rows]
        wide_grad = grad.astype(F32)
        use = ([0] if c % 2 else []) + ([1] if c >= 2 else [])
        for level in use:
            scaled = (wide[level, rows] * wide_grad).astype(BF16)
            value = mm(q, scaled, TN)
            if level == 0:
                near_grad[c - 1] = value
            else:
                pair_grad = value if pair_grad is None else pair_grad + value
    for c in range(tiles):
        rows = pl.ds(c * SUB, SUB)
        q, k, v, grad = q_ref[0, rows], k_ref[0, rows], v_ref[0, rows], g_ref[0, rows]
        wide_grad = grad.astype(F32)
        score = mm(q, k, NT)
        back = mm(grad, v, NT)
        wsum[c] += score * back
        weight = diag[c]
        weighted = (weight * score).astype(BF16)
        dscore = (weight * back).astype(BF16)
        out = mm(weighted, v, NN)
        qg = mm(dscore, k, NN)
        kg = mm(dscore, q, TN)
        vg = mm(weighted, grad, TN)
        use = ([0] if c % 2 else []) + ([1] if c >= 2 else []) + [2, 3, 4, 5, 6]
        buckets = ([near[c]] if c % 2 else []) + ([pair] if c >= 2 else []) + [far_bucket]
        joined = jnp.concatenate(buckets, axis=1)
        cross = mm(q, joined, NN)
        scaled = []
        for n, level in enumerate(use):
            piece = cross[:, n * 128 : (n + 1) * 128]
            lam = wide[level, rows]
            out += lam * piece
            lsum[level, rows] += piece * wide_grad
            scaled.append((lam * wide_grad).astype(BF16))
        qg += mm(jnp.concatenate(scaled, axis=1), joined, NT)
        dstate = far_grad
        if c in near_grad:
            dstate = dstate + near_grad[c]
        if c < 2:
            dstate = dstate + pair_grad
        dstate = dstate.astype(BF16)
        kg += mm(v, dstate, NT)
        vg += mm(k, dstate, NN)
        out_ref[0, rows] = out.astype(BF16)
        qg_ref[0, rows] = qg.astype(BF16)
        kg_ref[0, rows] = kg.astype(BF16)
        vg_ref[0, rows] = vg.astype(BF16)

    @pl.when(head == pl.num_programs(0) - 1)
    def _():
        hot = one_hot(index_ref[...], table_ref.shape[0])
        lane = lax.broadcasted_iota(jnp.int32, part_ref.shape, 1)
        rows = lax.broadcasted_iota(jnp.int32, (SUB, SUB), 0)
        cols = lax.broadcasted_iota(jnp.int32, (SUB, SUB), 1)
        crossed = jnp.bitwise_xor(rows, cols)
        table = jnp.zeros(part_ref.shape, F32)
        for level in range(16):
            if level < 9:
                total = jnp.zeros((table_ref.shape[0], 128), F32)
                low = (1 << (level - 1)) if level else 0
                mask = (crossed >= low) & (crossed < (1 << level)) & (cols <= rows)
                for c in range(tiles):
                    value = jnp.where(mask, wsum[c], 0.0)
                    value = value[:, :128] + value[:, 128:]
                    high, rest, _ = split3(value)
                    part = hot[:, c * SUB : (c + 1) * SUB]
                    total += mm(part, high, NN) + mm(part, rest, NN)
            else:
                high, rest, _ = split3(lsum[level - 9])
                total = mm(hot, high, NN) + mm(hot, rest, NN)
            column = jnp.sum(total, axis=1, keepdims=True)
            table = jnp.where(lane == level, column, table)
        part_ref[...] = table * factor


def body(queries, keys, values, out_grad, level_table, table_index):
    heads, length, width = queries.shape
    devices = lax.axis_size("ctx")
    factor = 1.0 / math.sqrt(width * length * devices)
    index_row = table_index.reshape(1, length)
    block = pl.BlockSpec((1, length, width), lambda h: (h, 0, 0))
    whole = lambda shape: pl.BlockSpec(shape, lambda h: (0,) * len(shape))
    scratch = [
        pltpu.VMEM((7, length, 128), F32),
        pltpu.VMEM((length // SUB, SUB, SUB), F32),
    ]
    params = pltpu.CompilerParams(
        dimension_semantics=("arbitrary",), vmem_limit_bytes=60 << 20
    )
    states, grads = pl.pallas_call(
        functools.partial(pre_kernel, factor=factor),
        grid=(heads,),
        out_shape=(
            jax.ShapeDtypeStruct((heads, width, width), F32),
            jax.ShapeDtypeStruct((5, heads, width, width), F32),
        ),
        in_specs=[block] * 4 + [whole(index_row.shape), whole(level_table.shape)],
        out_specs=(
            pl.BlockSpec((1, width, width), lambda h: (h, 0, 0)),
            pl.BlockSpec((5, 1, width, width), lambda h: (0, h, 0, 0)),
        ),
        scratch_shapes=scratch,
        compiler_params=params,
    )(queries, keys, values, out_grad, index_row, level_table)
    block_id = lax.axis_index("ctx")
    steps = (1, 2, 6, 8, 24)
    swap = lambda value, step: lax.ppermute(value, "ctx", [(b, b ^ step) for b in range(devices)])
    tree = states
    pieces = []
    dtree = jnp.zeros_like(states)
    received = [None] * 5
    for j, step in enumerate(steps):
        other = swap(tree, step)
        pieces.append(jnp.where((block_id >> j) & 1 == 1, other, 0.0))
        tree = tree + other
        back = 4 - j
        dtree = dtree + swap(dtree + grads[back], steps[back])
    bucket = jnp.concatenate(pieces, axis=-1)
    outs = pl.pallas_call(
        functools.partial(main_kernel, factor=factor),
        grid=(heads,),
        out_shape=tuple(jax.ShapeDtypeStruct(queries.shape, BF16) for _ in range(4))
        + (jax.ShapeDtypeStruct(level_table.shape, F32),),
        in_specs=[block] * 4
        + [
            whole(index_row.shape),
            whole(level_table.shape),
            pl.BlockSpec((1, width, 5 * width), lambda h: (h, 0, 0)),
            pl.BlockSpec((1, width, width), lambda h: (h, 0, 0)),
        ],
        out_specs=(block,) * 4 + (whole(level_table.shape),),
        scratch_shapes=scratch
        + [
            pltpu.VMEM((length // SUB, SUB, SUB), F32),
            pltpu.VMEM((7, length, 128), F32),
        ],
        compiler_params=params,
    )(queries, keys, values, out_grad, index_row, level_table, bucket, dtree)
    table_total = lax.psum(outs[4], ("ctx", "heads"))
    table_grad = table_total / math.sqrt(length * devices)
    return outs[:4] + (table_grad,)


def solution(mesh):
    placed = (P("heads", "ctx", None),) * 4
    return jax.shard_map(
        body,
        mesh=mesh,
        in_specs=placed + (P(), P("ctx")),
        out_specs=placed + (P(),),
        check_vma=False,
    )
```

time: 376 us -> 195 us (0.52); the launches traced: 370 us -> 194 us
  matrix products: 154 us -> 0 us
  Pallas kernels: 0 us -> 36.3 us
  other arithmetic: 50.8 us -> 18.9 us
  local copies, waits for them, and re-layouts: 22.4 us -> 5.42 us
  waiting for transfers between devices: 62.8 us -> 46.4 us
  starting transfers between devices: 0.25 us -> 15.7 us
  between operations: 14.6 us -> 0.68 us
  blocking collectives: 64.7 us -> 70.5 us
    dot_general x16 -> x0, matrix products: 154 us -> none  [the longest x1 30.6 us: block_finish(): jnp.einsum('htd,hsd->hts', queries, keys, preferred_element_type=jnp.floa...]
    all_gather x1 -> x0, waiting for transfers between devices: 62.7 us -> none  [body(): shard_piece = lax.all_gather(states[None], 'ctx', axis=0, tiled=True)]
    ppermute x0 -> x10, waiting for transfers between devices: none -> 46.4 us  [body(): lax.ppermute(value, 'ctx', [(b, b ^ step) for b in range(devices)])]
    pallas_call x0 -> x2, Pallas kernels: none -> 36.3 us  [the longest x1 26.1 us: body(): pl.pallas_call(functools.partial(main_kernel, factor=factor), grid=(heads...]
    reduce_sum x4 -> x0, other arithmetic: 31.6 us -> none  [the longest x1 18.2 us: block_finish(): jnp.sum(jnp.where(causal & (levels == level_id), weight_grad, 0.0), 1)]
    ppermute x0 -> x10, starting transfers between devices: none -> 15.7 us  [body(): lax.ppermute(value, 'ctx', [(b, b ^ step) for b in range(devices)])]
    reduce_sum x7 -> x0, local copies, waits for them, and re-layouts: 13 us -> none  [the longest x1 5.42 us: block_finish(): query_grad = query_local + factor * jnp.sum(lam_cross * back_cross, 0)]
    add x1 -> x9, other arithmetic: 8.71 us -> 18.8 us  [the longest x5 10.5 us: body(): dtree = dtree + swap(dtree + grads[back], steps[back])]
  transfers between devices with their start and end apart: 2 -> 10, of which waited for: 1 -> 6; matrix products, arithmetic and copies ran while one was open for 35% -> 10% of each run, Pallas kernels for 0% -> 0%
where the time goes in v1:
time: 195 us; the launch traced here: 194 us
  blocking collectives  70.5 us (36%)
  waiting for transfers between devices  46.4 us (24%)
  Pallas kernels  36.3 us (19%)
  other arithmetic  18.9 us (10%)
  starting transfers between devices  15.7 us (8%)
  local copies, waits for them, and re-layouts  5.42 us (3%)
    psum x1, blocking collectives, body(): table_total = lax.psum(outs[4], ('ctx', 'heads'))  70.5 us
    ppermute x10, waiting for transfers between devices, body(): lax.ppermute(value, 'ctx', [(b, b ^ step) for b in range(devices)])  46.4 us
    pallas_call x1, Pallas kernels, body(): pl.pallas_call(functools.partial(main_kernel, factor=factor), grid=(heads...  26.1 us
    ppermute x10, starting transfers between devices, body(): lax.ppermute(value, 'ctx', [(b, b ^ step) for b in range(devices)])  15.7 us
    add x5, other arithmetic, body(): dtree = dtree + swap(dtree + grads[back], steps[back])  10.5 us
    pallas_call x1, Pallas kernels, body(): pl.pallas_call(functools.partial(pre_kernel, factor=factor), grid=(heads,...  10.2 us
    add x4, other arithmetic, body(): tree = tree + other  8.29 us
    unnamed x6, local copies, waits for them, and re-layouts  4.35 us
  transfers between devices with their start and end apart: 10, of which 6 were waited for; matrix products, arithmetic and copies ran while one was open for 10% of the time, Pallas kernels for 0%

profile of v1, /device:TPU:1, one launch (start us, length us, event | category | flops | bytes accessed | tf_op | source)
XLA Modules:
  0.0 193.9 jit_solution(9853850307025326128)
XLA Ops:
  0.6 1.4 copy.12.table_ref
  2.0 10.2 %shard_map.101 = (f32[8,128,128]{2,1,0:T(8,128)}, f32[5,8,128,128]{3,2,1,0:T(8,128)}) custom-call(bf16[8,1024,128]{2,1,0:T(8,128)(2,1)} %q_ref.3, bf16[8,1024,128]{2,1,0:T(8,128)(2,1)} %k_ref.3, bf16[8,1024,128]{2,1,0:T(8,128)(2,1)} %v_ref.3, bf16[8,1024,128]{2,1,0:T(8,128)(2,1)} %g_ref.3, s32[1,1024]{1,0:T(1,128)} %bitcast.11, f32[64,16]{1,0:T(8,128)} %copy.12.table_ref), custom_call_target="tpu_custom_call" | custom-call | tf_op jit(solution)/shard_map/pallas_call | solution.py:186
  12.2 1.1 slice_bitcast_fusion
  13.3 3.4 %collective-permute-start.5 = (f32[8,128,128]{2,1,0:T(8,128)S(1)}, f32[8,128,128]{2,1,0:T(8,128)S(1)}, u32[]{:S(2)}, u32[]{:S(2)}) collective-permute-start(f32[8,128,128]{2,1,0:T(8,128)S(1)} %slice_bitcast_fusion), channel_id=1, source_target_pairs={{0,96},{4,100},{8,104},{12,108},{16,112},{20,116},{24,120},{28,124... | collective-permute-start | bytes 1572872 | tf_op jit(solution)/shard_map/ppermute | solution.py:203
  16.7 1.0 collective-permute-start
  17.6 10.3 %collective-permute-done.5 = f32[8,128,128]{2,1,0:T(8,128)S(1)} collective-permute-done((f32[8,128,128]{2,1,0:T(8,128)S(1)}, f32[8,128,128]{2,1,0:T(8,128)S(1)}, u32[]{:S(2)}, u32[]{:S(2)}) %collective-permute-start.5) | collective-permute-done | bytes 524320 | tf_op jit(solution)/shard_map/ppermute | solution.py:203
  27.9 1.9 bitcast_add_fusion.3
  29.8 0.3 collective-permute-start.6
  30.1 0.0 collective-permute-done
  30.1 2.1 %fusion.3 = (f32[8,128,128]{2,1,0:T(8,128)}, f32[8,128,640]{2,1,0:T(8,128)S(1)}) fusion(f32[8,128,128]{2,1,0:T(8,128)} %get-tuple-element.12, f32[8,128,128]{2,1,0:T(8,128)} %collective-permute-done, pred[]{:T(512)S(6)} %eq.15), kind=kLoop, calls=%fused_computation.14 | loop fusion | flops 262143 | bytes 2097153 | tf_op jit(solution)/shard_map/add | solution.py:211
  32.2 1.3 collective-permute-start.1
  33.5 8.5 %collective-permute-done.6 = f32[8,128,128]{2,1,0:T(8,128)} collective-permute-done((f32[8,128,128]{2,1,0:T(8,128)}, f32[8,128,128]{2,1,0:T(8,128)}, u32[]{:S(2)}, u32[]{:S(2)}) %collective-permute-start.6) | collective-permute-done | bytes 524320 | tf_op jit(solution)/shard_map/ppermute | solution.py:203
  42.0 2.3 %bitcast_add_fusion.2 = (f32[8,128,128]{2,1,0:T(8,128)}, f32[8,128,128]{2,1,0:T(8,128)}) fusion(f32[5,8,128,128]{3,2,1,0:T(8,128)} %get-tuple-element.13, f32[8,128,128]{2,1,0:T(8,128)S(1)} %collective-permute-done.5, f32[8,128,128]{2,1,0:T(8,128)} %collective-permute-done.6), kind=kLoop, calls=%fused_computation.2 | loop fusion | flops 262144 | bytes 2621440 | tf_op jit(solution)/shard_map/add | solution.py:213
  44.3 3.1 %collective-permute-start.7 = (f32[8,128,128]{2,1,0:T(8,128)}, f32[8,128,128]{2,1,0:T(8,128)S(1)}, u32[]{:S(2)}, u32[]{:S(2)}) collective-permute-start(f32[8,128,128]{2,1,0:T(8,128)} %get-tuple-element.28), channel_id=1, source_target_pairs={{0,24},{4,28},{8,16},{12,20},{16,8},{20,12},{24,0},{28,4},{32,56},... | collective-permute-start | bytes 1572872 | tf_op jit(solution)/shard_map/ppermute | solution.py:203
  47.4 0.0 collective-permute-done.1
  47.4 2.1 %fusion.2 = (f32[8,128,128]{2,1,0:T(8,128)}, f32[8,128,640]{2,1,0:T(8,128)S(1)}) fusion(f32[8,128,128]{2,1,0:T(8,128)} %get-tuple-element.36, f32[8,128,128]{2,1,0:T(8,128)} %collective-permute-done.1, f32[8,128,640]{2,1,0:T(8,128)S(1)} %get-tuple-element.37, pred[]{:T(512)S(6)} %eq.16), kind=kLoop, calls=%fused_computation.13 | loop fusion | flops 262144 | bytes 2097153 | tf_op jit(solution)/shard_map/add | solution.py:211
  49.4 0.0 collective-permute-start.2
  49.4 8.1 %collective-permute-done.7 = f32[8,128,128]{2,1,0:T(8,128)S(1)} collective-permute-done((f32[8,128,128]{2,1,0:T(8,128)}, f32[8,128,128]{2,1,0:T(8,128)S(1)}, u32[]{:S(2)}, u32[]{:S(2)}) %collective-permute-start.7) | collective-permute-done | bytes 524320 | tf_op jit(solution)/shard_map/ppermute | solution.py:203
  57.5 0.0 copy-start.1
  57.5 0.8 copy-done.1
  58.3 2.2 %bitcast_add_fusion.1 = (f32[8,128,128]{2,1,0:T(8,128)}, f32[8,128,128]{2,1,0:T(8,128)S(1)}) fusion(f32[5,8,128,128]{3,2,1,0:T(8,128)} %get-tuple-element.13, f32[8,128,128]{2,1,0:T(8,128)} %get-tuple-element.29, f32[8,128,128]{2,1,0:T(8,128)} %copy-done.1), kind=kLoop, calls=%fused_computation.1 | loop fusion | flops 262144 | bytes 2621440 | tf_op jit(solution)/shard_map/add | solution.py:213
  60.5 0.0 collective-permute-start.8
  60.5 8.3 %collective-permute-done.2 = f32[8,128,128]{2,1,0:T(8,128)} collective-permute-done((f32[8,128,128]{2,1,0:T(8,128)}, f32[8,128,128]{2,1,0:T(8,128)}, u32[]{:S(2)}, u32[]{:S(2)}) %collective-permute-start.2) | collective-permute-done | bytes 524320 | tf_op jit(solution)/shard_map/ppermute | solution.py:203
  68.8 2.1 %fusion.1 = (f32[8,128,128]{2,1,0:T(8,128)}, f32[8,128,640]{2,1,0:T(8,128)S(1)}) fusion(f32[8,128,128]{2,1,0:T(8,128)} %get-tuple-element.34, f32[8,128,128]{2,1,0:T(8,128)} %collective-permute-done.2, f32[8,128,640]{2,1,0:T(8,128)S(1)} %get-tuple-element.35, pred[]{:T(512)S(6)} %eq.17), kind=kLoop, calls=%fused_computation.12 | loop fusion | flops 262144 | bytes 2097153 | tf_op jit(solution)/shard_map/add | solution.py:211
  70.9 0.0 collective-permute-start.3
  70.9 0.0 collective-permute-done.8
  70.9 2.3 %bitcast_add_fusion = (f32[8,128,128]{2,1,0:T(8,128)}, f32[8,128,128]{2,1,0:T(8,128)}) fusion(f32[5,8,128,128]{3,2,1,0:T(8,128)} %get-tuple-element.13, f32[8,128,128]{2,1,0:T(8,128)S(1)} %get-tuple-element.27, f32[8,128,128]{2,1,0:T(8,128)} %collective-permute-done.8), kind=kLoop, calls=%fused_computation | loop fusion | flops 262144 | bytes 2621440 | tf_op jit(solution)/shard_map/add | solution.py:213
  73.2 4.6 %collective-permute-start.9 = (f32[8,128,128]{2,1,0:T(8,128)}, f32[8,128,128]{2,1,0:T(8,128)S(1)}, u32[]{:S(2)}, u32[]{:S(2)}) collective-permute-start(f32[8,128,128]{2,1,0:T(8,128)} %get-tuple-element.24), channel_id=1, source_target_pairs={{0,4},{4,0},{8,12},{12,8},{16,20},{20,16},{24,28},{28,24},{32,36},... | collective-permute-start | bytes 1572872 | tf_op jit(solution)/shard_map/ppermute | solution.py:203
  77.8 3.9 %collective-permute-done.3 = f32[8,128,128]{2,1,0:T(8,128)} collective-permute-done((f32[8,128,128]{2,1,0:T(8,128)}, f32[8,128,128]{2,1,0:T(8,128)}, u32[]{:S(2)}, u32[]{:S(2)}) %collective-permute-start.3) | collective-permute-done | bytes 524320 | tf_op jit(solution)/shard_map/ppermute | solution.py:203
  81.7 2.1 %fusion = (f32[8,128,128]{2,1,0:T(8,128)}, f32[8,128,640]{2,1,0:T(8,128)S(1)}) fusion(f32[8,128,128]{2,1,0:T(8,128)} %get-tuple-element.32, f32[8,128,128]{2,1,0:T(8,128)} %collective-permute-done.3, f32[8,128,640]{2,1,0:T(8,128)S(1)} %get-tuple-element.33, pred[]{:T(512)S(6)} %eq.18), kind=kLoop, calls=%fused_computation.11 | loop fusion | flops 262144 | bytes 2097153 | tf_op jit(solution)/shard_map/add | solution.py:211
  83.8 2.1 %collective-permute-start.4 = (f32[8,128,128]{2,1,0:T(8,128)}, f32[8,128,128]{2,1,0:T(8,128)}, u32[]{:S(2)}, u32[]{:S(2)}) collective-permute-start(f32[8,128,128]{2,1,0:T(8,128)} %get-tuple-element.30), channel_id=1, source_target_pairs={{0,96},{4,100},{8,104},{12,108},{16,112},{20,116},{24,120},{28,124... | collective-permute-start | bytes 1572872 | tf_op jit(solution)/shard_map/ppermute | solution.py:203
  85.9 0.0 collective-permute-done.9
  85.9 1.9 add.49.sgrad_ref
  87.8 7.2 %collective-permute-done.4 = f32[8,128,128]{2,1,0:T(8,128)} collective-permute-done((f32[8,128,128]{2,1,0:T(8,128)}, f32[8,128,128]{2,1,0:T(8,128)}, u32[]{:S(2)}, u32[]{:S(2)}) %collective-permute-start.4) | collective-permute-done | bytes 524320 | tf_op jit(solution)/shard_map/ppermute | solution.py:203
  95.0 0.0 copy-start
  95.1 1.5 copy-done
  96.5 26.1 %shard_map.102 = (bf16[8,1024,128]{2,1,0:T(8,128)(2,1)}, bf16[8,1024,128]{2,1,0:T(8,128)(2,1)}, bf16[8,1024,128]{2,1,0:T(8,128)(2,1)}, bf16[8,1024,128]{2,1,0:T(8,128)(2,1)}, f32[64,16]{1,0:T(8,128)}) custom-call(bf16[8,1024,128]{2,1,0:T(8,128)(2,1)} %q_ref.3, bf16[8,1024,128]{2,1,0:T(8,128)(2,1)} %k_ref.3, bf16[8,1024,128]{2,1,0:T(8,128)(2,1)} %v_ref.3, ...), custom_call_target="tpu_custom_call" | custom-call | tf_op jit(solution)/shard_map/pallas_call | solution.py:215
  122.7 70.5 %psum.7 = f32[64,16]{1,0:T(8,128)S(1)} all-reduce(f32[64,16]{1,0:T(8,128)} %get-tuple-element.18), channel_id=1, replica_groups=mesh['ctx'=32,'heads'=4] {'ctx','heads'}, use_global_device_ids=true, to_apply=%region_0.1 | all-reduce | flops 1024 | bytes 8192 | tf_op jit(solution)/shard_map/psum | solution.py:235
  193.2 0.7 copy.13
  (2 shorter events, 0.0 us)
Async XLA Ops:
  13.3 14.6 %collective-permute-start.5 = (f32[8,128,128]{2,1,0:T(8,128)S(1)}, f32[8,128,128]{2,1,0:T(8,128)S(1)}, u32[]{:S(2)}, u32[]{:S(2)}) collective-permute-start(f32[8,128,128]{2,1,0:T(8,128)S(1)} %slice_bitcast_fusion), channel_id=1, source_target_pairs={{0,96},{4,100},{8,104},{12,108},{16,112},{20,116},{24,120},{28,124... | collective-permute-start | bytes 1572872 | tf_op jit(solution)/shard_map/ppermute | solution.py:203
  16.7 13.4 %collective-permute-start = (f32[8,128,128]{2,1,0:T(8,128)}, f32[8,128,128]{2,1,0:T(8,128)}, u32[]{:S(2)}, u32[]{:S(2)}) collective-permute-start(f32[8,128,128]{2,1,0:T(8,128)} %get-tuple-element.12), channel_id=1, source_target_pairs={{0,4},{4,0},{8,12},{12,8},{16,20},{20,16},{24,28},{28,24},{32,36},... | collective-permute-start | bytes 1572872 | tf_op jit(solution)/shard_map/ppermute | solution.py:203
  29.8 12.2 %collective-permute-start.6 = (f32[8,128,128]{2,1,0:T(8,128)}, f32[8,128,128]{2,1,0:T(8,128)}, u32[]{:S(2)}, u32[]{:S(2)}) collective-permute-start(f32[8,128,128]{2,1,0:T(8,128)} %bitcast_add_fusion.3), channel_id=1, source_target_pairs={{0,32},{4,36},{8,40},{12,44},{16,48},{20,52},{24,56},{28,60},{32,0... | collective-permute-start | bytes 1572872 | tf_op jit(solution)/shard_map/ppermute | solution.py:203
  32.2 15.2 %collective-permute-start.1 = (f32[8,128,128]{2,1,0:T(8,128)}, f32[8,128,128]{2,1,0:T(8,128)}, u32[]{:S(2)}, u32[]{:S(2)}) collective-permute-start(f32[8,128,128]{2,1,0:T(8,128)} %get-tuple-element.36), channel_id=1, source_target_pairs={{0,8},{4,12},{8,0},{12,4},{16,24},{20,28},{24,16},{28,20},{32,40},... | collective-permute-start | bytes 1572872 | tf_op jit(solution)/shard_map/ppermute | solution.py:203
  44.3 13.2 %collective-permute-start.7 = (f32[8,128,128]{2,1,0:T(8,128)}, f32[8,128,128]{2,1,0:T(8,128)S(1)}, u32[]{:S(2)}, u32[]{:S(2)}) collective-permute-start(f32[8,128,128]{2,1,0:T(8,128)} %get-tuple-element.28), channel_id=1, source_target_pairs={{0,24},{4,28},{8,16},{12,20},{16,8},{20,12},{24,0},{28,4},{32,56},... | collective-permute-start | bytes 1572872 | tf_op jit(solution)/shard_map/ppermute | solution.py:203
  49.4 19.4 %collective-permute-start.2 = (f32[8,128,128]{2,1,0:T(8,128)}, f32[8,128,128]{2,1,0:T(8,128)}, u32[]{:S(2)}, u32[]{:S(2)}) collective-permute-start(f32[8,128,128]{2,1,0:T(8,128)} %get-tuple-element.34), channel_id=1, source_target_pairs={{0,24},{4,28},{8,16},{12,20},{16,8},{20,12},{24,0},{28,4},{32,56},... | collective-permute-start | bytes 1572872 | tf_op jit(solution)/shard_map/ppermute | solution.py:203
  57.5 0.8 copy-start.1
  60.5 10.4 %collective-permute-start.8 = (f32[8,128,128]{2,1,0:T(8,128)}, f32[8,128,128]{2,1,0:T(8,128)}, u32[]{:S(2)}, u32[]{:S(2)}) collective-permute-start(f32[8,128,128]{2,1,0:T(8,128)} %get-tuple-element.26), channel_id=1, source_target_pairs={{0,8},{4,12},{8,0},{12,4},{16,24},{20,28},{24,16},{28,20},{32,40},... | collective-permute-start | bytes 1572872 | tf_op jit(solution)/shard_map/ppermute | solution.py:203
  70.9 10.8 %collective-permute-start.3 = (f32[8,128,128]{2,1,0:T(8,128)}, f32[8,128,128]{2,1,0:T(8,128)}, u32[]{:S(2)}, u32[]{:S(2)}) collective-permute-start(f32[8,128,128]{2,1,0:T(8,128)} %get-tuple-element.32), channel_id=1, source_target_pairs={{0,32},{4,36},{8,40},{12,44},{16,48},{20,52},{24,56},{28,60},{32,0... | collective-permute-start | bytes 1572872 | tf_op jit(solution)/shard_map/ppermute | solution.py:203
  73.2 12.7 %collective-permute-start.9 = (f32[8,128,128]{2,1,0:T(8,128)}, f32[8,128,128]{2,1,0:T(8,128)S(1)}, u32[]{:S(2)}, u32[]{:S(2)}) collective-permute-start(f32[8,128,128]{2,1,0:T(8,128)} %get-tuple-element.24), channel_id=1, source_target_pairs={{0,4},{4,0},{8,12},{12,8},{16,20},{20,16},{24,28},{28,24},{32,36},... | collective-permute-start | bytes 1572872 | tf_op jit(solution)/shard_map/ppermute | solution.py:203
  83.8 11.2 %collective-permute-start.4 = (f32[8,128,128]{2,1,0:T(8,128)}, f32[8,128,128]{2,1,0:T(8,128)}, u32[]{:S(2)}, u32[]{:S(2)}) collective-permute-start(f32[8,128,128]{2,1,0:T(8,128)} %get-tuple-element.30), channel_id=1, source_target_pairs={{0,96},{4,100},{8,104},{12,108},{16,112},{20,116},{24,120},{28,124... | collective-permute-start | bytes 1572872 | tf_op jit(solution)/shard_map/ppermute | solution.py:203
  95.0 1.5 copy-start

commit v2 on v0

v2 whole, which is shorter than its diff:
```python
import functools
import math

import jax
import jax.numpy as jnp
from jax import lax
from jax.experimental import pallas as pl
from jax.experimental.pallas import tpu as pltpu
from jax.sharding import PartitionSpec as P

SUB = 256
PIECES = 2
MESH = pl.DeviceIdType.MESH
F32 = jnp.float32
BF16 = jnp.bfloat16
NN = (((1,), (0,)), ((), ()))
NT = (((1,), (1,)), ((), ()))
TN = (((0,), (0,)), ((), ()))
TT = (((0,), (1,)), ((), ()))


def mm(a, b, dims):
    return lax.dot_general(a, b, dims, preferred_element_type=F32)


def split3(value):
    first = value.astype(BF16)
    rest = value - first.astype(F32)
    second = rest.astype(BF16)
    third = (rest - second.astype(F32)).astype(BF16)
    return first, second, third


def one_hot(index_row, rows):
    length = index_row.shape[1]
    row_ids = lax.broadcasted_iota(jnp.int32, (rows, length), 0)
    return jnp.where(row_ids == index_row, 1.0, 0.0).astype(BF16)


def fill_lambda(hot, table_ref, wide_ref, diag_ref, factor):
    parts = split3(table_ref[...] * factor)
    lam = sum(mm(hot, part, TT) for part in parts)
    length = lam.shape[0]
    for level in range(wide_ref.shape[0]):
        column = lam[:, 9 + level : 10 + level]
        wide_ref[level] = jnp.broadcast_to(column, (length, 128))
    rows = lax.broadcasted_iota(jnp.int32, (SUB, SUB), 0)
    cols = lax.broadcasted_iota(jnp.int32, (SUB, SUB), 1)
    crossed = jnp.bitwise_xor(rows, cols)
    for tile in range(length // SUB):
        part = lam[tile * SUB : (tile + 1) * SUB]
        weight = jnp.broadcast_to(part[:, 0:1], (SUB, SUB))
        for level in range(1, 9):
            weight = jnp.where(crossed >= 1 << (level - 1), part[:, level : level + 1], weight)
        diag_ref[tile] = jnp.where(cols <= rows, weight, 0.0)


def row_sums(hot, value):
    high, rest, _ = split3(value)
    total = mm(hot, high, NN) + mm(hot, rest, NN)
    return jnp.sum(total, axis=1, keepdims=True)


def kernel(
    q_hbm, k_hbm, v_hbm, g_hbm, index_ref, table_ref,
    out_hbm, qg_hbm, kg_hbm, vg_hbm, total_ref,
    qb, kb, vb, gb, lout, lq, lk, lv, wide, diag, wsum, lsum, near, part, cat,
    states, sother, grads, gother, g0other, tree, recv, dsend, drecv, dtree, psum,
    in_sem, out_sem, s_send, s_recv, g_send, g_recv, f_send, f_recv, r_send, r_recv,
    b_send, b_recv, d_send, d_recv, p_send, p_recv,
    *, factor, scale,
):
    heads, length, _ = qb.shape
    tiles = length // SUB
    half = heads // 2
    unit = half // PIECES
    me = lax.axis_index("ctx")
    z = lax.axis_index("heads")
    core = me % 2
    y = (me // 2) % 4
    x = me // 8
    mine = core * half
    theirs = (1 - core) * half
    sibling = me + 1 - 2 * core
    at = lambda px, py: (px * 4 + py) * 2 + core
    hops = (at(x, y + 1 - 2 * (y % 2)), at(x, 3 - y), at(x + 1 - 2 * (x % 2), y), at(3 - x, y))
    bits = (core == 1, y % 2 == 1, y // 2 == 1, x % 2 == 1, x // 2 == 1)

    def pick(level):
        return jnp.where(level == 0, hops[0], jnp.where(level == 1, hops[1], jnp.where(level == 2, hops[2], hops[3])))

    def remote(src, dst, send, got, device):
        return pltpu.make_async_remote_copy(
            src_ref=src, dst_ref=dst, send_sem=send, recv_sem=got, device_id=device, device_id_type=MESH
        )

    loads = ((kb, k_hbm), (vb, v_hbm), (qb, q_hbm), (gb, g_hbm))

    def load(n, h):
        return pltpu.make_async_copy(loads[n][1].at[h], loads[n][0].at[h], in_sem.at[n, h])

    def start_loads(first):
        def step(i, carry):
            h = lax.rem(theirs + i, heads)
            load(first, h).start()
            load(first + 1, h).start()
            return carry

        lax.fori_loop(0, heads, step, 0)

    start_loads(0)
    start_loads(2)

    barrier = pltpu.get_barrier_semaphore()
    pl.semaphore_signal(barrier, inc=1, device_id={"ctx": sibling}, device_id_type=MESH)
    for d in range(1, 4):
        pl.semaphore_signal(barrier, inc=1, device_id={"ctx": at(x, (y + d) % 4)}, device_id_type=MESH)
        pl.semaphore_signal(barrier, inc=1, device_id={"ctx": at((x + d) % 4, y)}, device_id_type=MESH)
        pl.semaphore_signal(barrier, inc=1, device_id={"heads": (z + d) % 4}, device_id_type=MESH)

    hot = one_hot(index_ref[...], table_ref.shape[1])
    fill_lambda(hot, table_ref, wide, diag, factor)

    def state_step(i, carry):
        h = lax.rem(theirs + i, heads)
        load(0, h).wait()
        load(1, h).wait()
        s = [mm(kb[h, pl.ds(c * SUB, SUB)], vb[h, pl.ds(c * SUB, SUB)], TN) for c in range(tiles)]
        pair = s[0] + s[1]
        near[h, 0] = s[0].astype(BF16)
        near[h, 1] = s[2].astype(BF16)
        near[h, 2] = pair.astype(BF16)
        states[h] = pair + (s[2] + s[3])
        return carry

    lax.fori_loop(0, heads, state_step, 0)
    pl.semaphore_wait(barrier, 10)

    def state_copy(n, low):
        block = pl.ds(low, half)
        return remote(states.at[block], sother.at[block], s_send.at[n], s_recv.at[n], {"ctx": sibling})

    state_copy(0, theirs).start()
    state_copy(1, mine).start()
    wsum[...] = jnp.zeros_like(wsum)
    lsum[...] = jnp.zeros_like(lsum)

    def grad_step(i, carry):
        h = lax.rem(theirs + i, heads)
        load(2, h).wait()
        load(3, h).wait()
        total = None
        for c in range(tiles):
            rows = pl.ds(c * SUB, SUB)
            wide_grad = gb[h, rows].astype(F32)
            scaled = jnp.concatenate([(wide[2 + j, rows] * wide_grad).astype(BF16) for j in range(5)], axis=1)
            value = mm(qb[h, rows], scaled, TN)
            total = value if total is None else total + value
        for j in range(5):
            grads[j, h] = jnp.where(bits[j], total[:, j * 128 : (j + 1) * 128], 0.0)
        return carry

    def tree_copy(level, u):
        src = tree.at[level, pl.ds(u * unit, unit)]
        dst = recv.at[level, pl.ds(mine + u * unit, unit)]
        return remote(src, dst, f_send.at[level, u], f_recv.at[level, u], {"ctx": pick(level)})

    def relay(level, u, low):
        block = recv.at[level, pl.ds(low + u * unit, unit)]
        return remote(block, block, r_send.at[level, u], r_recv.at[level, u], {"ctx": sibling})

    def dtree_copy(level, u):
        block = pl.ds(u * unit, unit)
        return remote(dsend.at[level, block], drecv.at[level, block], b_send.at[level, u], b_recv.at[level, u], {"ctx": pick(level)})

    def dtree_relay(u, low):
        block = dtree.at[pl.ds(low + u * unit, unit)]
        return remote(block, block, d_send.at[u], d_recv.at[u], {"ctx": sibling})

    def grad_copy(j):
        return remote(grads.at[j, pl.ds(theirs, half)], gother.at[j - 1], g_send.at[j], g_recv.at[j], {"ctx": sibling})

    def grad0_copy():
        return remote(grads.at[0], g0other, g_send.at[0], g_recv.at[0], {"ctx": sibling})

    lax.fori_loop(0, half, grad_step, 0)
    state_copy(0, mine).wait_recv()
    tree[0] = states[pl.ds(mine, half)] + sother[pl.ds(mine, half)]
    for j in (4, 3, 2, 1):
        grad_copy(j).start()
    for u in range(PIECES):
        tree_copy(0, u).start()
    lax.fori_loop(half, heads, grad_step, 0)
    grad0_copy().start()
    grad_copy(4).wait_recv()
    dsend[3] = grads[4, pl.ds(mine, half)] + gother[3]
    for u in range(PIECES):
        dtree_copy(3, u).start()

    def comm_step(step):
        level = step // PIECES
        u = step % PIECES
        back = 3 - level
        block = pl.ds(u * unit, unit)
        own = pl.ds(mine + u * unit, unit)

        @pl.when((u == 0) & (level < 3))
        def _():
            grad_copy(back).wait_recv()

        tree_copy(level, u).wait_recv()
        relay(level, u, mine).start()
        dtree_copy(back, u).wait_recv()

        @pl.when(level < 3)
        def _():
            tree[level + 1, block] = tree[level, block] + recv[level, own]

        @pl.when(level == 0)
        def _():
            dtree[own] = drecv[back, block]

        @pl.when(level > 0)
        def _():
            dtree[own] = dtree[own] + drecv[back, block]

        @pl.when(level < 3)
        def _():
            dsend[back - 1, block] = dtree[own] + (grads[back, own] + gother[back - 1, block])
            tree_copy(level + 1, u).start()
            dtree_copy(back - 1, u).start()

        @pl.when(level == 3)
        def _():
            dtree_relay(u, mine).start()

    def local_head(h):
        def tile(c):
            rows = pl.ds(c * SUB, SUB)
            return rows, qb[h, rows], kb[h, rows], vb[h, rows], gb[h, rows]

        near_grad = {}
        pair_grad = None
        for c in range(tiles - 1, -1, -1):
            rows, q, k, v, grad = tile(c)
            score = mm(q, k, NT)
            back = mm(grad, v, NT)
            wsum[c] += score * back
            weight = diag[c]
            weighted = (weight * score).astype(BF16)
            dscore = (weight * back).astype(BF16)
            out = mm(weighted, v, NN)
            qg = mm(dscore, k, NN)
            kg = mm(dscore, q, TN)
            vg = mm(weighted, grad, TN)
            use = ([0] if c % 2 else []) + ([1] if c >= 2 else [])
            if use:
                buckets = ([near[h, c // 2]] if c % 2 else []) + ([near[h, 2]] if c >= 2 else [])
                joined = jnp.concatenate(buckets, axis=1)
                cross = mm(q, joined, NN)
                wide_grad = grad.astype(F32)
                scaled = []
                for n, level in enumerate(use):
                    piece = cross[:, n * 128 : (n + 1) * 128]
                    lam = wide[level, rows]
                    out += lam * piece
                    lsum[level, rows] += piece * wide_grad
                    scaled.append((lam * wide_grad).astype(BF16))
                scaled = jnp.concatenate(scaled, axis=1)
                qg += mm(scaled, joined, NT)
                value = mm(q, scaled, TN)
                for n, level in enumerate(use):
                    piece = value[:, n * 128 : (n + 1) * 128]
                    if level == 0:
                        near_grad[c - 1] = piece
                    else:
                        pair_grad = piece if pair_grad is None else pair_grad + piece
            dstate = near_grad.get(c)
            if c < 2:
                dstate = pair_grad if dstate is None else dstate + pair_grad
            if dstate is not None:
                dlocal[c] = dstate
            lout[h, rows] = out
            lq[h, rows] = qg
            lk[h, rows] = kg
            lv[h, rows] = vg
        return dlocal

    dlocal = {}

    def local_step(h, carry):
        @pl.when(h > 0)
        def _():
            comm_step(h - 1)

        local_head(h)
        for c in range(3):
            part[h, c] = dlocal[c]
        return carry

    lax.fori_loop(0, heads, local_step, 0)

    lane = lax.broadcasted_iota(jnp.int32, (table_ref.shape[1], 128), 1)
    hot = one_hot(index_ref[...], table_ref.shape[1])
    rows_id = lax.broadcasted_iota(jnp.int32, (SUB, SUB), 0)
    cols_id = lax.broadcasted_iota(jnp.int32, (SUB, SUB), 1)
    crossed = jnp.bitwise_xor(rows_id, cols_id)
    table = jnp.zeros(lane.shape, F32)
    for level in range(11):
        if level < 9:
            low = (1 << (level - 1)) if level else 0
            mask = (crossed >= low) & (crossed < (1 << level)) & (cols_id <= rows_id)
            values = []
            for c in range(tiles):
                value = jnp.where(mask, wsum[c], 0.0)
                values.append(value[:, :128] + value[:, 128:])
            value = jnp.concatenate(values, axis=0)
        else:
            value = lsum[level - 9]
        table = jnp.where(lane == level, row_sums(hot, value), table)

    for step in range(heads - 1, 4 * PIECES):
        comm_step(step)

    state_copy(1, theirs).wait_recv()
    for level in range(4):
        for u in range(PIECES):
            relay(level, u, theirs).wait_recv()

    stores = ((qb, out_hbm), (gb, qg_hbm), (vb, kg_hbm), (kb, vg_hbm))

    def store(n, h):
        return pltpu.make_async_copy(stores[n][0].at[h], stores[n][1].at[h], out_sem.at[n, h])

    def cross_step(h, carry):
        cat[h, :, 0:128] = jnp.where(bits[0], sother[h], 0.0).astype(BF16)
        for j in range(1, 5):
            cat[h, :, j * 128 : (j + 1) * 128] = jnp.where(bits[j], recv[j - 1, h], 0.0).astype(BF16)
        joined = cat[h]
        for c in range(tiles):
            rows = pl.ds(c * SUB, SUB)
            cross = mm(qb[h, rows], joined, NN)
            wide_grad = gb[h, rows].astype(F32)
            out = lout[h, rows]
            for j in range(5):
                piece = cross[:, j * 128 : (j + 1) * 128]
                out += wide[2 + j, rows] * piece
                lsum[2 + j, rows] += piece * wide_grad
            qb[h, rows] = out.astype(BF16)
        store(0, h).start()
        return carry

    lax.fori_loop(0, heads, cross_step, 0)
    for level in range(11, 16):
        table = jnp.where(lane == level, row_sums(hot, lsum[level - 9]), table)

    spots = (z, y, x)
    psum[0, z, :, 0:64] = (table * scale).T[0:16]

    def table_copy(phase, d):
        spot = spots[phase]
        other = (spot + d) % 4
        device = (
            {"heads": other},
            {"ctx": at(x, other)},
            {"ctx": at(other, y)},
        )[phase]
        return remote(
            psum.at[phase, spot], psum.at[phase, spot], p_send.at[phase, d - 1], p_recv.at[phase, d - 1], device
        )

    def table_wait(phase, d):
        other = (spots[phase] + 4 - d) % 4
        slot = psum.at[phase, other]
        return remote(slot, slot, p_send.at[phase, d - 1], p_recv.at[phase, d - 1], {"ctx": sibling})

    def core_copy():
        return remote(psum.at[3, core], psum.at[3, core], p_send.at[3, 0], p_recv.at[3, 0], {"ctx": sibling})

    def core_wait():
        slot = psum.at[3, 1 - core]
        return remote(slot, slot, p_send.at[3, 0], p_recv.at[3, 0], {"ctx": sibling})

    for d in range(1, 4):
        table_copy(0, d).start()

    def table_phase(phase):
        for d in range(1, 4):
            table_wait(phase, d).wait_recv()
        value = (psum[phase, 0] + psum[phase, 1]) + (psum[phase, 2] + psum[phase, 3])
        if phase < 2:
            psum[phase + 1, spots[phase + 1]] = value
            for d in range(1, 4):
                table_copy(phase + 1, d).start()
        else:
            psum[3, core] = value
            core_copy().start()

    for u in range(PIECES):
        dtree_relay(u, theirs).wait_recv()
    grad0_copy().wait_recv()

    def grad_head(h):
        joined = cat[h]
        far = dtree[h] + jnp.where(bits[0], 0.0, g0other[h])
        for c in range(tiles):
            rows = pl.ds(c * SUB, SUB)
            wide_grad = gb[h, rows].astype(F32)
            scaled = jnp.concatenate([(wide[2 + j, rows] * wide_grad).astype(BF16) for j in range(5)], axis=1)
            qg = lq[h, rows] + mm(scaled, joined, NT)
            dstate = (far + part[h, c] if c < 3 else far).astype(BF16)
            kg = lk[h, rows] + mm(vb[h, rows], dstate, NT)
            vg = lv[h, rows] + mm(kb[h, rows], dstate, NN)
            gb[h, rows] = qg.astype(BF16)
            vb[h, rows] = kg.astype(BF16)
            kb[h, rows] = vg.astype(BF16)
        for n in range(1, 4):
            store(n, h).start()

    def grad_loop(low, high):
        def step(h, carry):
            grad_head(h)
            return carry

        lax.fori_loop(low, high, step, 0)

    grad_loop(0, 3)
    table_phase(0)
    grad_loop(3, 6)
    table_phase(1)
    grad_loop(6, heads)
    table_phase(2)
    core_wait().wait_recv()
    total_ref[...] = (psum[3, 0] + psum[3, 1])[:, 0:64]

    def drain(h, carry):
        for n in range(4):
            store(n, h).wait()
        return carry

    lax.fori_loop(0, heads, drain, 0)
    state_copy(0, theirs).wait_send()
    state_copy(1, mine).wait_send()
    grad0_copy().wait_send()
    for j in range(1, 5):
        grad_copy(j).wait_send()
    for u in range(PIECES):
        for level in range(4):
            tree_copy(level, u).wait_send()
            relay(level, u, mine).wait_send()
            dtree_copy(level, u).wait_send()
        dtree_relay(u, mine).wait_send()
    for phase in range(3):
        for d in range(1, 4):
            table_copy(phase, d).wait_send()
    core_copy().wait_send()


def body(queries, keys, values, out_grad, level_table, table_index):
    heads, length, width = queries.shape
    devices = lax.axis_size("ctx")
    factor = 1.0 / math.sqrt(width * length * devices)
    tiles = length // SUB
    half = heads // 2
    dma = lambda *shape: pltpu.SemaphoreType.DMA(shape)
    square = (width, width)
    outs = pl.pallas_call(
        functools.partial(kernel, factor=factor, scale=factor / math.sqrt(length * devices)),
        out_shape=tuple(jax.ShapeDtypeStruct(queries.shape, BF16) for _ in range(4))
        + (jax.ShapeDtypeStruct(level_table.shape[::-1], F32),),
        in_specs=[pl.BlockSpec(memory_space=pltpu.HBM)] * 4 + [pl.BlockSpec(memory_space=pltpu.VMEM)] * 2,
        out_specs=(pl.BlockSpec(memory_space=pltpu.HBM),) * 4 + (pl.BlockSpec(memory_space=pltpu.VMEM),),
        scratch_shapes=[pltpu.VMEM(queries.shape, BF16)] * 4
        + [pltpu.VMEM(queries.shape, F32)] * 4
        + [
            pltpu.VMEM((7, length, 128), F32),
            pltpu.VMEM((tiles, SUB, SUB), F32),
            pltpu.VMEM((tiles, SUB, SUB), F32),
            pltpu.VMEM((7, length, 128), F32),
            pltpu.VMEM((heads, 3) + square, BF16),
            pltpu.VMEM((heads, 3) + square, F32),
            pltpu.VMEM((heads, width, 5 * width), BF16),
            pltpu.VMEM((heads,) + square, F32),
            pltpu.VMEM((heads,) + square, F32),
            pltpu.VMEM((5, heads) + square, F32),
            pltpu.VMEM((4, half) + square, F32),
            pltpu.VMEM((heads,) + square, F32),
            pltpu.VMEM((4, half) + square, F32),
            pltpu.VMEM((4, heads) + square, F32),
            pltpu.VMEM((4, half) + square, F32),
            pltpu.VMEM((4, half) + square, F32),
            pltpu.VMEM((heads,) + square, F32),
            pltpu.VMEM((4, 4, 16, 128), F32),
            dma(4, heads), dma(4, heads), dma(2), dma(2), dma(5), dma(5),
            dma(4, PIECES), dma(4, PIECES), dma(4, PIECES), dma(4, PIECES),
            dma(4, PIECES), dma(4, PIECES), dma(PIECES), dma(PIECES), dma(4, 3), dma(4, 3),
        ],
        compiler_params=pltpu.CompilerParams(
            collective_id=0, has_side_effects=True, vmem_limit_bytes=67043328
        ),
    )(queries, keys, values, out_grad, table_index.reshape(1, length), level_table.T)
    return outs[:4] + (outs[4].T,)


def solution(mesh):
    placed = (P("heads", "ctx", None),) * 4
    return jax.shard_map(
        body,
        mesh=mesh,
        in_specs=placed + (P(), P("ctx")),
        out_specs=placed + (P(),),
        check_vma=False,
    )
```

time: 376 us -> 71 us (0.19); the launches traced: 370 us -> 70.8 us
  matrix products: 154 us -> 0 us
  blocking collectives: 64.7 us -> 0 us
  waiting for transfers between devices: 62.8 us -> 0 us
  Pallas kernels: 0 us -> 60.3 us
  other arithmetic: 50.8 us -> 0 us
  between operations: 14.6 us -> 0.65 us
  local copies, waits for them, and re-layouts: 22.4 us -> 9.83 us
    dot_general x16 -> x0, matrix products: 154 us -> none  [the longest x1 30.6 us: block_finish(): jnp.einsum('htd,hsd->hts', queries, keys, preferred_element_type=jnp.floa...]
    psum x1 -> x0, blocking collectives: 64.7 us -> none  [body(): table_total = lax.psum(table_part, ('ctx', 'heads'))]
    all_gather x1 -> x0, waiting for transfers between devices: 62.7 us -> none  [body(): shard_piece = lax.all_gather(states[None], 'ctx', axis=0, tiled=True)]
    pallas_call x0 -> x1, Pallas kernels: none -> 60.3 us  [body(): pl.pallas_call(functools.partial(kernel, factor=factor, scale=factor / ma...]
    reduce_sum x4 -> x0, other arithmetic: 31.6 us -> none  [the longest x1 18.2 us: block_finish(): jnp.sum(jnp.where(causal & (levels == level_id), weight_grad, 0.0), 1)]
    reduce_sum x7 -> x0, local copies, waits for them, and re-layouts: 13 us -> none  [the longest x1 5.42 us: block_finish(): query_grad = query_local + factor * jnp.sum(lam_cross * back_cross, 0)]
    mul x8 -> x0, other arithmetic: 9.65 us -> none  [the longest x1 9.62 us: block_finish(): weight = factor * jnp.where(causal, weight, 0.0)]
    add x1 -> x0, other arithmetic: 8.71 us -> none  [body(): term + jnp.where(member[:, None, None, None], grads[bit_num][None], 0.0)]
  transfers between devices with their start and end apart: 2 -> 0, of which waited for: 1 -> 0; matrix products, arithmetic and copies ran while one was open for 35% -> 0% of each run, Pallas kernels for 0% -> 0%
where the time goes in v2:
time: 71 us; the launch traced here: 70.8 us
  Pallas kernels  60.3 us (85%)
  local copies, waits for them, and re-layouts  9.83 us (14%)
    pallas_call x1, Pallas kernels, body(): pl.pallas_call(functools.partial(kernel, factor=factor, scale=factor / ma...  60.3 us
    unnamed x13, local copies, waits for them, and re-layouts  9.83 us

profile of v2, /device:TPU:1, one launch (start us, length us, event | category | flops | bytes accessed | tf_op | source)
XLA Modules:
  0.0 70.8 jit_solution(15470893426118816759)
XLA Ops:
  0.6 60.3 %shard_map.101 = (bf16[8,1024,128]{2,1,0:T(8,128)(2,1)}, bf16[8,1024,128]{2,1,0:T(8,128)(2,1)}, bf16[8,1024,128]{2,1,0:T(8,128)(2,1)}, bf16[8,1024,128]{2,1,0:T(8,128)(2,1)}, f32[16,64]{1,0:T(8,128)}) custom-call(bf16[8,1024,128]{2,1,0:T(8,128)(2,1)} %q_hbm.1, bf16[8,1024,128]{2,1,0:T(8,128)(2,1)} %k_hbm.1, bf16[8,1024,128]{2,1,0:T(8,128)(2,1)} %v_hbm.1, ...), custom_call_target="tpu_custom_call" | custom-call | tf_op jit(solution)/shard_map/pallas_call | solution.py:467
  60.9 0.0 copy-start.2
  61.0 3.2 %copy.16 = bf16[8,1024,128]{2,1,0:T(8,128)(2,1)} copy(bf16[8,1024,128]{2,1,0:T(8,128)(2,1)} %get-tuple-element.20) | data formatting | bytes 4194304
  64.2 0.0 copy-done.2
  64.2 0.0 copy-start.1
  64.2 1.3 %copy.17 = bf16[8,1024,128]{2,1,0:T(8,128)(2,1)} copy(bf16[8,1024,128]{2,1,0:T(8,128)(2,1)S(1)} %copy-done.2) | data formatting | bytes 4194304
  65.5 1.0 %copy-done.1 = bf16[8,1024,128]{2,1,0:T(8,128)(2,1)S(1)} copy-done((bf16[8,1024,128]{2,1,0:T(8,128)(2,1)S(1)}, bf16[8,1024,128]{2,1,0:T(8,128)(2,1)}, u32[]{:S(2)}) %copy-start.1) | copy-done | bytes 2097176
  66.5 0.0 copy-start
  66.5 1.3 %copy.18 = bf16[8,1024,128]{2,1,0:T(8,128)(2,1)} copy(bf16[8,1024,128]{2,1,0:T(8,128)(2,1)S(1)} %copy-done.1) | data formatting | bytes 4194304
  67.8 1.0 %copy-done = bf16[8,1024,128]{2,1,0:T(8,128)(2,1)S(1)} copy-done((bf16[8,1024,128]{2,1,0:T(8,128)(2,1)S(1)}, bf16[8,1024,128]{2,1,0:T(8,128)(2,1)}, u32[]{:S(2)}) %copy-start) | copy-done | bytes 2097176
  68.9 0.0 copy-start.3
  68.9 1.3 %copy.19 = bf16[8,1024,128]{2,1,0:T(8,128)(2,1)} copy(bf16[8,1024,128]{2,1,0:T(8,128)(2,1)S(1)} %copy-done) | data formatting | bytes 4194304
  70.2 0.0 copy-done.3
  70.2 0.6 copy.20
Async XLA Ops:
  60.9 3.2 %copy-start.2 = (bf16[8,1024,128]{2,1,0:T(8,128)(2,1)S(1)}, bf16[8,1024,128]{2,1,0:T(8,128)(2,1)}, u32[]{:S(2)}) copy-start(bf16[8,1024,128]{2,1,0:T(8,128)(2,1)} %get-tuple-element.21) | copy-start | bytes 6291460
  64.2 2.3 %copy-start.1 = (bf16[8,1024,128]{2,1,0:T(8,128)(2,1)S(1)}, bf16[8,1024,128]{2,1,0:T(8,128)(2,1)}, u32[]{:S(2)}) copy-start(bf16[8,1024,128]{2,1,0:T(8,128)(2,1)} %get-tuple-element.22) | copy-start | bytes 6291460
  66.5 2.3 %copy-start = (bf16[8,1024,128]{2,1,0:T(8,128)(2,1)S(1)}, bf16[8,1024,128]{2,1,0:T(8,128)(2,1)}, u32[]{:S(2)}) copy-start(bf16[8,1024,128]{2,1,0:T(8,128)(2,1)} %get-tuple-element.23) | copy-start | bytes 6291460
  68.9 1.3 %copy-start.3 = (f32[16,64]{1,0:T(8,128)S(1)}, f32[16,64]{1,0:T(8,128)}, u32[]{:S(2)}) copy-start(f32[16,64]{1,0:T(8,128)} %get-tuple-element.14) | copy-start | bytes 12292

commit v3 on v2

--- a/solution.py
+++ b/solution.py
@@ -9,7 +9,8 @@
 from jax.sharding import PartitionSpec as P
 
 SUB = 256
-PIECES = 2
+PARTNERS = 13
+TREE_LAG = 1
 MESH = pl.DeviceIdType.MESH
 F32 = jnp.float32
 BF16 = jnp.bfloat16
@@ -63,17 +64,16 @@
 
 def kernel(
     q_hbm, k_hbm, v_hbm, g_hbm, index_ref, table_ref,
-    out_hbm, qg_hbm, kg_hbm, vg_hbm, total_ref,
+    out_ref, qg_ref, kg_ref, vg_ref, total_ref,
     qb, kb, vb, gb, lout, lq, lk, lv, wide, diag, wsum, lsum, near, part, cat,
     states, sother, grads, gother, g0other, tree, recv, dsend, drecv, dtree, psum,
-    in_sem, out_sem, s_send, s_recv, g_send, g_recv, f_send, f_recv, r_send, r_recv,
+    in_sem, s_send, s_recv, g_send, g_recv, f_send, f_recv, r_send, r_recv,
     b_send, b_recv, d_send, d_recv, p_send, p_recv,
     *, factor, scale,
 ):
     heads, length, _ = qb.shape
     tiles = length // SUB
     half = heads // 2
-    unit = half // PIECES
     me = lax.axis_index("ctx")
     z = lax.axis_index("heads")
     core = me % 2
@@ -99,30 +99,25 @@
     def load(n, h):
         return pltpu.make_async_copy(loads[n][1].at[h], loads[n][0].at[h], in_sem.at[n, h])
 
-    def start_loads(first):
-        def step(i, carry):
-            h = lax.rem(theirs + i, heads)
-            load(first, h).start()
-            load(first + 1, h).start()
-            return carry
-
-        lax.fori_loop(0, heads, step, 0)
-
-    start_loads(0)
-    start_loads(2)
+    def load_pair(n, h):
+        load(n, h).start()
+        load(n + 1, h).start()
+
+    for n in (0, 2):
+        for u in range(half):
+            load_pair(n, theirs + u)
+            load_pair(n, mine + u)
 
     barrier = pltpu.get_barrier_semaphore()
-    pl.semaphore_signal(barrier, inc=1, device_id={"ctx": sibling}, device_id_type=MESH)
     for d in range(1, 4):
         pl.semaphore_signal(barrier, inc=1, device_id={"ctx": at(x, (y + d) % 4)}, device_id_type=MESH)
         pl.semaphore_signal(barrier, inc=1, device_id={"ctx": at((x + d) % 4, y)}, device_id_type=MESH)
-        pl.semaphore_signal(barrier, inc=1, device_id={"heads": (z + d) % 4}, device_id_type=MESH)
-
-    hot = one_hot(index_ref[...], table_ref.shape[1])
-    fill_lambda(hot, table_ref, wide, diag, factor)
-
-    def state_step(i, carry):
-        h = lax.rem(theirs + i, heads)
+    for d in range(1, 8):
+        spot = (z * 2 + core + d) % 8
+        device = {"ctx": me - core + spot % 2, "heads": spot // 2}
+        pl.semaphore_signal(barrier, inc=1, device_id=device, device_id_type=MESH)
+
+    def make_state(h):
         load(0, h).wait()
         load(1, h).wait()
         s = [mm(kb[h, pl.ds(c * SUB, SUB)], vb[h, pl.ds(c * SUB, SUB)], TN) for c in range(tiles)]
@@ -131,22 +126,16 @@
         near[h, 1] = s[2].astype(BF16)
         near[h, 2] = pair.astype(BF16)
         states[h] = pair + (s[2] + s[3])
-        return carry
-
-    lax.fori_loop(0, heads, state_step, 0)
-    pl.semaphore_wait(barrier, 10)
-
-    def state_copy(n, low):
+
+    def state_copy(u, low):
+        block = states.at[low + u]
+        return remote(block, sother.at[low + u], s_send.at[u], s_recv.at[u], {"ctx": sibling})
+
+    def rest_copy(low):
         block = pl.ds(low, half)
-        return remote(states.at[block], sother.at[block], s_send.at[n], s_recv.at[n], {"ctx": sibling})
-
-    state_copy(0, theirs).start()
-    state_copy(1, mine).start()
-    wsum[...] = jnp.zeros_like(wsum)
-    lsum[...] = jnp.zeros_like(lsum)
-
-    def grad_step(i, carry):
-        h = lax.rem(theirs + i, heads)
+        return remote(states.at[block], sother.at[block], s_send.at[half], s_recv.at[half], {"ctx": sibling})
+
+    def make_grad(h):
         load(2, h).wait()
         load(3, h).wait()
         total = None
@@ -158,83 +147,117 @@
             total = value if total is None else total + value
         for j in range(5):
             grads[j, h] = jnp.where(bits[j], total[:, j * 128 : (j + 1) * 128], 0.0)
-        return carry
 
     def tree_copy(level, u):
-        src = tree.at[level, pl.ds(u * unit, unit)]
-        dst = recv.at[level, pl.ds(mine + u * unit, unit)]
-        return remote(src, dst, f_send.at[level, u], f_recv.at[level, u], {"ctx": pick(level)})
+        return remote(
+            tree.at[level, u], recv.at[level, mine + u], f_send.at[level, u], f_recv.at[level, u], {"ctx": pick(level)}
+        )
 
     def relay(level, u, low):
-        block = recv.at[level, pl.ds(low + u * unit, unit)]
+        block = recv.at[level, low + u]
         return remote(block, block, r_send.at[level, u], r_recv.at[level, u], {"ctx": sibling})
 
     def dtree_copy(level, u):
-        block = pl.ds(u * unit, unit)
-        return remote(dsend.at[level, block], drecv.at[level, block], b_send.at[level, u], b_recv.at[level, u], {"ctx": pick(level)})
+        return remote(
+            dsend.at[level, u], drecv.at[level, u], b_send.at[level, u], b_recv.at[level, u], {"ctx": pick(level)}
+        )
 
     def dtree_relay(u, low):
-        block = dtree.at[pl.ds(low + u * unit, unit)]
+        block = dtree.at[low + u]
         return remote(block, block, d_send.at[u], d_recv.at[u], {"ctx": sibling})
 
-    def grad_copy(j):
-        return remote(grads.at[j, pl.ds(theirs, half)], gother.at[j - 1], g_send.at[j], g_recv.at[j], {"ctx": sibling})
+    def grad_copy(u):
+        return remote(grads.at[pl.ds(1, 4), theirs + u], gother.at[:, u], g_send.at[u], g_recv.at[u], {"ctx": sibling})
 
     def grad0_copy():
-        return remote(grads.at[0], g0other, g_send.at[0], g_recv.at[0], {"ctx": sibling})
-
-    lax.fori_loop(0, half, grad_step, 0)
-    state_copy(0, mine).wait_recv()
-    tree[0] = states[pl.ds(mine, half)] + sother[pl.ds(mine, half)]
-    for j in (4, 3, 2, 1):
-        grad_copy(j).start()
-    for u in range(PIECES):
+        return remote(grads.at[0], g0other, g_send.at[half], g_recv.at[half], {"ctx": sibling})
+
+    def start_tree(u):
+        state_copy(u, mine).wait_recv()
+        tree[0, u] = states[mine + u] + sother[mine + u]
         tree_copy(0, u).start()
-    lax.fori_loop(half, heads, grad_step, 0)
-    grad0_copy().start()
-    grad_copy(4).wait_recv()
-    dsend[3] = grads[4, pl.ds(mine, half)] + gother[3]
-    for u in range(PIECES):
+
+    def start_dtree(u):
+        grad_copy(u).wait_recv()
+        dsend[3, u] = grads[4, mine + u] + gother[3, u]
         dtree_copy(3, u).start()
 
-    def comm_step(step):
-        level = step // PIECES
-        u = step % PIECES
-        back = 3 - level
-        block = pl.ds(u * unit, unit)
-        own = pl.ds(mine + u * unit, unit)
-
-        @pl.when((u == 0) & (level < 3))
-        def _():
-            grad_copy(back).wait_recv()
-
+    def tree_step(step):
+        level = step // half
+        u = step % half
         tree_copy(level, u).wait_recv()
         relay(level, u, mine).start()
+
+        @pl.when(level < 3)
+        def _():
+            tree[level + 1, u] = tree[level, u] + recv[level, mine + u]
+            tree_copy(level + 1, u).start()
+
+    def dtree_step(step):
+        level = step // half
+        u = step % half
+        back = 3 - level
         dtree_copy(back, u).wait_recv()
 
+        @pl.when(level == 0)
+        def _():
+            dtree[mine + u] = drecv[back, u]
+
+        @pl.when(level > 0)
+        def _():
+            dtree[mine + u] = dtree[mine + u] + drecv[back, u]
+
         @pl.when(level < 3)
         def _():
-            tree[level + 1, block] = tree[level, block] + recv[level, own]
-
-        @pl.when(level == 0)
-        def _():
-            dtree[own] = drecv[back, block]
-
-        @pl.when(level > 0)
-        def _():
-            dtree[own] = dtree[own] + drecv[back, block]
-
-        @pl.when(level < 3)
-        def _():
-            dsend[back - 1, block] = dtree[own] + (grads[back, own] + gother[back - 1, block])
-            tree_copy(level + 1, u).start()
+            dsend[back - 1, u] = dtree[mine + u] + (grads[back, mine + u] + gother[back - 1, u])
             dtree_copy(back - 1, u).start()
 
         @pl.when(level == 3)
         def _():
             dtree_relay(u, mine).start()
 
-    def local_head(h):
+    def state_step(u, carry):
+        make_state(theirs + u)
+
+        @pl.when(u == 0)
+        def _():
+            pl.semaphore_wait(barrier, PARTNERS)
+
+        state_copy(u, theirs).start()
+        make_state(mine + u)
+
+        @pl.when(u >= 2)
+        def _():
+            start_tree(u - 2)
+
+        return carry
+
+    lax.fori_loop(0, half, state_step, 0)
+    rest_copy(mine).start()
+    start_tree(2)
+    wsum[...] = jnp.zeros_like(wsum)
+    lsum[...] = jnp.zeros_like(lsum)
+    start_tree(3)
+    hot = one_hot(index_ref[...], table_ref.shape[1])
+    fill_lambda(hot, table_ref, wide, diag, factor)
+
+    def grad_step(u, carry):
+        make_grad(theirs + u)
+        grad_copy(u).start()
+        make_grad(mine + u)
+
+        @pl.when(u >= 1)
+        def _():
+            start_dtree(u - 1)
+
+        tree_step(u)
+        return carry
+
+    lax.fori_loop(0, half, grad_step, 0)
+    grad0_copy().start()
+    start_dtree(3)
+
+    def local_head(h, between):
         def tile(c):
             rows = pl.ds(c * SUB, SUB)
             return rows, qb[h, rows], kb[h, rows], vb[h, rows], gb[h, rows]
@@ -242,6 +265,8 @@
         near_grad = {}
         pair_grad = None
         for c in range(tiles - 1, -1, -1):
+            if c == 1:
+                between()
             rows, q, k, v, grad = tile(c)
             score = mm(q, k, NT)
             back = mm(grad, v, NT)
@@ -289,13 +314,19 @@
     dlocal = {}
 
     def local_step(h, carry):
-        @pl.when(h > 0)
-        def _():
-            comm_step(h - 1)
-
-        local_head(h)
+        def comm_step(step):
+            @pl.when((step >= TREE_LAG) & (step < TREE_LAG + 3 * half))
+            def _():
+                tree_step(step - TREE_LAG + half)
+
+            @pl.when(step >= half)
+            def _():
+                dtree_step(step - half)
+
+        local_head(h, lambda: comm_step(2 * h))
         for c in range(3):
             part[h, c] = dlocal[c]
+        comm_step(2 * h + 1)
         return carry
 
     lax.fori_loop(0, heads, local_step, 0)
@@ -319,18 +350,10 @@
             value = lsum[level - 9]
         table = jnp.where(lane == level, row_sums(hot, value), table)
 
-    for step in range(heads - 1, 4 * PIECES):
-        comm_step(step)
-
-    state_copy(1, theirs).wait_recv()
+    rest_copy(theirs).wait_recv()
     for level in range(4):
-        for u in range(PIECES):
+        for u in range(half):
             relay(level, u, theirs).wait_recv()
-
-    stores = ((qb, out_hbm), (gb, qg_hbm), (vb, kg_hbm), (kb, vg_hbm))
-
-    def store(n, h):
-        return pltpu.make_async_copy(stores[n][0].at[h], stores[n][1].at[h], out_sem.at[n, h])
 
     def cross_step(h, carry):
         cat[h, :, 0:128] = jnp.where(bits[0], sother[h], 0.0).astype(BF16)
@@ -346,57 +369,54 @@
                 piece = cross[:, j * 128 : (j + 1) * 128]
                 out += wide[2 + j, rows] * piece
                 lsum[2 + j, rows] += piece * wide_grad
-            qb[h, rows] = out.astype(BF16)
-        store(0, h).start()
+            out_ref[h, rows] = out.astype(BF16)
+
+        @pl.when(h % 2 == 1)
+        def _():
+            dtree_step(3 * half + h // 2)
+
         return carry
 
     lax.fori_loop(0, heads, cross_step, 0)
     for level in range(11, 16):
         table = jnp.where(lane == level, row_sums(hot, lsum[level - 9]), table)
 
-    spots = (z, y, x)
-    psum[0, z, :, 0:64] = (table * scale).T[0:16]
+    spots = (z * 2 + core, y, x)
+    sizes = (8, 4, 4)
+    psum[0, spots[0]] = (table * scale).T[0:16]
 
     def table_copy(phase, d):
-        spot = spots[phase]
-        other = (spot + d) % 4
+        other = (spots[phase] + d) % sizes[phase]
         device = (
-            {"heads": other},
+            {"ctx": at(x, y) - core + other % 2, "heads": other // 2},
             {"ctx": at(x, other)},
             {"ctx": at(other, y)},
         )[phase]
-        return remote(
-            psum.at[phase, spot], psum.at[phase, spot], p_send.at[phase, d - 1], p_recv.at[phase, d - 1], device
-        )
+        slot = psum.at[phase, spots[phase]]
+        return remote(slot, slot, p_send.at[phase, d - 1], p_recv.at[phase, d - 1], device)
 
     def table_wait(phase, d):
-        other = (spots[phase] + 4 - d) % 4
+        other = (spots[phase] + sizes[phase] - d) % sizes[phase]
         slot = psum.at[phase, other]
         return remote(slot, slot, p_send.at[phase, d - 1], p_recv.at[phase, d - 1], {"ctx": sibling})
 
-    def core_copy():
-        return remote(psum.at[3, core], psum.at[3, core], p_send.at[3, 0], p_recv.at[3, 0], {"ctx": sibling})
-
-    def core_wait():
-        slot = psum.at[3, 1 - core]
-        return remote(slot, slot, p_send.at[3, 0], p_recv.at[3, 0], {"ctx": sibling})
-
-    for d in range(1, 4):
+    for d in range(1, 8):
         table_copy(0, d).start()
 
     def table_phase(phase):
-        for d in range(1, 4):
+        for d in range(1, sizes[phase]):
             table_wait(phase, d).wait_recv()
-        value = (psum[phase, 0] + psum[phase, 1]) + (psum[phase, 2] + psum[phase, 3])
+        value = psum[phase, 0]
+        for n in range(1, sizes[phase]):
+            value = value + psum[phase, n]
         if phase < 2:
             psum[phase + 1, spots[phase + 1]] = value
             for d in range(1, 4):
                 table_copy(phase + 1, d).start()
         else:
-            psum[3, core] = value
-            core_copy().start()
-
-    for u in range(PIECES):
+            total_ref[...] = value[:, 0:64]
+
+    for u in range(half):
         dtree_relay(u, theirs).wait_recv()
     grad0_copy().wait_recv()
 
@@ -411,11 +431,9 @@
             dstate = (far + part[h, c] if c < 3 else far).astype(BF16)
             kg = lk[h, rows] + mm(vb[h, rows], dstate, NT)
             vg = lv[h, rows] + mm(kb[h, rows], dstate, NN)
-            gb[h, rows] = qg.astype(BF16)
-            vb[h, rows] = kg.astype(BF16)
-            kb[h, rows] = vg.astype(BF16)
-        for n in range(1, 4):
-            store(n, h).start()
+            qg_ref[h, rows] = qg.astype(BF16)
+            kg_ref[h, rows] = kg.astype(BF16)
+            vg_ref[h, rows] = vg.astype(BF16)
 
     def grad_loop(low, high):
         def step(h, carry):
@@ -430,30 +448,36 @@
     table_phase(1)
     grad_loop(6, heads)
     table_phase(2)
-    core_wait().wait_recv()
-    total_ref[...] = (psum[3, 0] + psum[3, 1])[:, 0:64]
-
-    def drain(h, carry):
-        for n in range(4):
-            store(n, h).wait()
-        return carry
-
-    lax.fori_loop(0, heads, drain, 0)
-    state_copy(0, theirs).wait_send()
-    state_copy(1, mine).wait_send()
+
+    rest_copy(mine).wait_send()
     grad0_copy().wait_send()
-    for j in range(1, 5):
-        grad_copy(j).wait_send()
-    for u in range(PIECES):
+    for u in range(half):
+        state_copy(u, theirs).wait_send()
+        grad_copy(u).wait_send()
         for level in range(4):
             tree_copy(level, u).wait_send()
             relay(level, u, mine).wait_send()
             dtree_copy(level, u).wait_send()
         dtree_relay(u, mine).wait_send()
     for phase in range(3):
-        for d in range(1, 4):
+        for d in range(1, sizes[phase]):
             table_copy(phase, d).wait_send()
-    core_copy().wait_send()
+
+
+def put_kernel(*refs):
+    sems = refs[-1]
+    count = (len(refs) - 1) // 2
+    copies = []
+    for n in range(count - 1):
+        for h in range(0, refs[n].shape[0], 2):
+            rows = pl.ds(h, 2)
+            copies.append((refs[n].at[rows], refs[count + n].at[rows]))
+    copies.append((refs[count - 1], refs[2 * count - 1]))
+    copies = [pltpu.make_async_copy(src, dst, sems.at[i]) for i, (src, dst) in enumerate(copies)]
+    for copy in copies:
+        copy.start()
+    for copy in copies:
+        copy.wait()
 
 
 def body(queries, keys, values, out_grad, level_table, table_index):
@@ -464,12 +488,13 @@
     half = heads // 2
     dma = lambda *shape: pltpu.SemaphoreType.DMA(shape)
     square = (width, width)
+    table_lanes = level_table.shape[0]
     outs = pl.pallas_call(
         functools.partial(kernel, factor=factor, scale=factor / math.sqrt(length * devices)),
-        out_shape=tuple(jax.ShapeDtypeStruct(queries.shape, BF16) for _ in range(4))
-        + (jax.ShapeDtypeStruct(level_table.shape[::-1], F32),),
+        out_shape=tuple(pltpu.VMEM(queries.shape, BF16) for _ in range(4))
+        + (pltpu.VMEM(level_table.shape[::-1], F32),),
         in_specs=[pl.BlockSpec(memory_space=pltpu.HBM)] * 4 + [pl.BlockSpec(memory_space=pltpu.VMEM)] * 2,
-        out_specs=(pl.BlockSpec(memory_space=pltpu.HBM),) * 4 + (pl.BlockSpec(memory_space=pltpu.VMEM),),
+        out_specs=(pl.BlockSpec(memory_space=pltpu.VMEM),) * 5,
         scratch_shapes=[pltpu.VMEM(queries.shape, BF16)] * 4
         + [pltpu.VMEM(queries.shape, F32)] * 4
         + [
@@ -490,15 +515,24 @@
             pltpu.VMEM((4, half) + square, F32),
             pltpu.VMEM((4, half) + square, F32),
             pltpu.VMEM((heads,) + square, F32),
-            pltpu.VMEM((4, 4, 16, 128), F32),
-            dma(4, heads), dma(4, heads), dma(2), dma(2), dma(5), dma(5),
-            dma(4, PIECES), dma(4, PIECES), dma(4, PIECES), dma(4, PIECES),
-            dma(4, PIECES), dma(4, PIECES), dma(PIECES), dma(PIECES), dma(4, 3), dma(4, 3),
+            pltpu.VMEM((3, 8, 16, table_lanes), F32),
+            dma(4, heads), dma(half + 1), dma(half + 1), dma(half + 1), dma(half + 1),
+            dma(4, half), dma(4, half), dma(4, half), dma(4, half),
+            dma(4, half), dma(4, half), dma(half), dma(half), dma(3, 7), dma(3, 7),
         ],
         compiler_params=pltpu.CompilerParams(
-            collective_id=0, has_side_effects=True, vmem_limit_bytes=67043328
+            collective_id=0, has_side_effects=True, vmem_limit_bytes=52 << 20
         ),
     )(queries, keys, values, out_grad, table_index.reshape(1, length), level_table.T)
+    outs = pl.pallas_call(
+        put_kernel,
+        out_shape=tuple(jax.ShapeDtypeStruct(queries.shape, BF16) for _ in range(4))
+        + (jax.ShapeDtypeStruct(level_table.shape[::-1], F32),),
+        in_specs=[pl.BlockSpec(memory_space=pltpu.VMEM)] * 5,
+        out_specs=(pl.BlockSpec(memory_space=pltpu.HBM),) * 5,
+        scratch_shapes=[dma(4 * heads // 2 + 1)],
+        compiler_params=pltpu.CompilerParams(vmem_limit_bytes=1 << 20),
+    )(*[pltpu.with_memory_space_constraint(value, pltpu.VMEM) for value in outs])
     return outs[:4] + (outs[4].T,)
 
 

time: 71 us -> 61.6 us (0.87)
  local copies, waits for them, and re-layouts: 9.83 us -> 0 us
    unnamed x13 -> x0, local copies, waits for them, and re-layouts: 9.83 us -> none
    pallas_call x1, Pallas kernels: 60.3 us -> 56.6 us  [body(): pl.pallas_call(functools.partial(kernel, factor=factor, scale=factor / ma...]
    pallas_call x0 -> x1, Pallas kernels: none -> 3.43 us  [body(): pl.pallas_call(put_kernel, out_shape=tuple((jax.ShapeDtypeStruct(queries....]
where the time goes in v3:
time: 61.6 us; the launch traced here: 60.7 us
  Pallas kernels  60.1 us (98%)
  between operations  0.64 us (1%)
    pallas_call x1, Pallas kernels, body(): pl.pallas_call(functools.partial(kernel, factor=factor, scale=factor / ma...  56.6 us
    pallas_call x1, Pallas kernels, body(): pl.pallas_call(put_kernel, out_shape=tuple((jax.ShapeDtypeStruct(queries....  3.43 us

profile of v3, /device:TPU:1, one launch (start us, length us, event | category | flops | bytes accessed | tf_op | source)
XLA Modules:
  0.0 60.7 jit_solution(5650622423442838690)
XLA Ops:
  0.6 56.6 %shard_map.101 = (bf16[8,1024,128]{2,1,0:T(8,128)(2,1)S(1)}, bf16[8,1024,128]{2,1,0:T(8,128)(2,1)S(1)}, bf16[8,1024,128]{2,1,0:T(8,128)(2,1)S(1)}, bf16[8,1024,128]{2,1,0:T(8,128)(2,1)S(1)}, f32[16,64]{1,0:T(8,128)S(1)}) custom-call(bf16[8,1024,128]{2,1,0:T(8,128)(2,1)} %q_hbm.1, bf16[8,1024,128]{2,1,0:T(8,128)(2,1)} %k_hbm.1, bf16[8,1024,128]{2,1,0:T(8,128)(2,1)} %v_hbm.1, ...), custom_call_target="tpu_custom_call" | custom-call | tf_op jit(solution)/shard_map/pallas_call | solution.py:492
  57.3 3.4 %shard_map.102 = (bf16[8,1024,128]{2,1,0:T(8,128)(2,1)}, bf16[8,1024,128]{2,1,0:T(8,128)(2,1)}, bf16[8,1024,128]{2,1,0:T(8,128)(2,1)}, bf16[8,1024,128]{2,1,0:T(8,128)(2,1)}, f32[16,64]{1,0:T(8,128)}) custom-call(bf16[8,1024,128]{2,1,0:T(8,128)(2,1)S(1)} %get-tuple-element.15.refs_0_, bf16[8,1024,128]{2,1,0:T(8,128)(2,1)S(1)} %get-tuple-element.16.refs_1_, ...), custom_call_target="tpu_custom_call" | custom-call | tf_op jit(solution)/shard_map/pallas_call | solution.py:527

commit v4 on v3

--- a/solution.py
+++ b/solution.py
@@ -9,8 +9,9 @@
 from jax.sharding import PartitionSpec as P
 
 SUB = 256
-PARTNERS = 13
+PARTNERS = 22
 TREE_LAG = 1
+DTREE_LAG = 4
 MESH = pl.DeviceIdType.MESH
 F32 = jnp.float32
 BF16 = jnp.bfloat16
@@ -39,21 +40,40 @@
 
 
 def fill_lambda(hot, table_ref, wide_ref, diag_ref, factor):
-    parts = split3(table_ref[...] * factor)
-    lam = sum(mm(hot, part, TT) for part in parts)
-    length = lam.shape[0]
+    table = (table_ref[...] * factor).T
+    hots = jnp.concatenate([hot, hot], axis=0)
+    length = hot.shape[1]
+
+    def wide_lams(level):
+        columns = jnp.concatenate(
+            [jnp.broadcast_to(table[:, n : n + 1], (table.shape[0], 128)) for n in (level, level + 1)], axis=1
+        )
+        value = mm(hots, jnp.concatenate(split3(columns)[:2], axis=0), TN)
+        return value[:, :128], value[:, 128:]
+
+    lams = [lam for level in range(0, 16, 2) for lam in wide_lams(level)]
     for level in range(wide_ref.shape[0]):
-        column = lam[:, 9 + level : 10 + level]
-        wide_ref[level] = jnp.broadcast_to(column, (length, 128))
-    rows = lax.broadcasted_iota(jnp.int32, (SUB, SUB), 0)
-    cols = lax.broadcasted_iota(jnp.int32, (SUB, SUB), 1)
+        wide_ref[level] = lams[9 + level]
+    rows = lax.broadcasted_iota(jnp.int32, (128, 128), 0)
+    cols = lax.broadcasted_iota(jnp.int32, (128, 128), 1)
     crossed = jnp.bitwise_xor(rows, cols)
+    for level in range(8):
+        lam = lams[level]
+        for n in range(length // 128):
+            tile, half = n // 2, n % 2
+            spot = pl.ds(half * 128, 128)
+            part = lam[n * 128 : (n + 1) * 128]
+            if level == 0:
+                diag_ref[tile, spot, spot] = jnp.where(cols <= rows, part, 0.0)
+            else:
+                low = 1 << (level - 1)
+                diag_ref[tile, spot, spot] = jnp.where(
+                    (crossed >= low) & (cols <= rows), part, diag_ref[tile, spot, spot]
+                )
+    lam = lams[8]
     for tile in range(length // SUB):
-        part = lam[tile * SUB : (tile + 1) * SUB]
-        weight = jnp.broadcast_to(part[:, 0:1], (SUB, SUB))
-        for level in range(1, 9):
-            weight = jnp.where(crossed >= 1 << (level - 1), part[:, level : level + 1], weight)
-        diag_ref[tile] = jnp.where(cols <= rows, weight, 0.0)
+        diag_ref[tile, 0:128, 128:256] = jnp.zeros((128, 128), F32)
+        diag_ref[tile, 128:256, 0:128] = lam[tile * SUB + 128 : (tile + 1) * SUB]
 
 
 def row_sums(hot, value):
@@ -65,7 +85,7 @@
 def kernel(
     q_hbm, k_hbm, v_hbm, g_hbm, index_ref, table_ref,
     out_ref, qg_ref, kg_ref, vg_ref, total_ref,
-    qb, kb, vb, gb, lout, lq, lk, lv, wide, diag, wsum, lsum, near, part, cat,
+    qb, kb, vb, gb, lout, lq, lk, lv, wide, diag, wsum, lsum, near, part, stack, pa, da, pb, db,
     states, sother, grads, gother, g0other, tree, recv, dsend, drecv, dtree, psum,
     in_sem, s_send, s_recv, g_send, g_recv, f_send, f_recv, r_send, r_recv,
     b_send, b_recv, d_send, d_recv, p_send, p_recv,
@@ -109,9 +129,9 @@
             load_pair(n, mine + u)
 
     barrier = pltpu.get_barrier_semaphore()
-    for d in range(1, 4):
-        pl.semaphore_signal(barrier, inc=1, device_id={"ctx": at(x, (y + d) % 4)}, device_id_type=MESH)
-        pl.semaphore_signal(barrier, inc=1, device_id={"ctx": at((x + d) % 4, y)}, device_id_type=MESH)
+    for d in range(1, 16):
+        spot = (x * 4 + y + d) % 16
+        pl.semaphore_signal(barrier, inc=1, device_id={"ctx": at(spot // 4, spot % 4)}, device_id_type=MESH)
     for d in range(1, 8):
         spot = (z * 2 + core + d) % 8
         device = {"ctx": me - core + spot % 2, "heads": spot // 2}
@@ -135,18 +155,16 @@
         block = pl.ds(low, half)
         return remote(states.at[block], sother.at[block], s_send.at[half], s_recv.at[half], {"ctx": sibling})
 
-    def make_grad(h):
-        load(2, h).wait()
-        load(3, h).wait()
+    def make_grad(h, low, high):
         total = None
         for c in range(tiles):
             rows = pl.ds(c * SUB, SUB)
             wide_grad = gb[h, rows].astype(F32)
-            scaled = jnp.concatenate([(wide[2 + j, rows] * wide_grad).astype(BF16) for j in range(5)], axis=1)
+            scaled = jnp.concatenate([(wide[2 + j, rows] * wide_grad).astype(BF16) for j in range(low, high)], axis=1)
             value = mm(qb[h, rows], scaled, TN)
             total = value if total is None else total + value
-        for j in range(5):
-            grads[j, h] = jnp.where(bits[j], total[:, j * 128 : (j + 1) * 128], 0.0)
+        for j in range(low, high):
+            grads[j, h] = jnp.where(bits[j], total[:, (j - low) * 128 : (j - low + 1) * 128], 0.0)
 
     def tree_copy(level, u):
         return remote(
@@ -166,11 +184,14 @@
         block = dtree.at[low + u]
         return remote(block, block, d_send.at[u], d_recv.at[u], {"ctx": sibling})
 
-    def grad_copy(u):
-        return remote(grads.at[pl.ds(1, 4), theirs + u], gother.at[:, u], g_send.at[u], g_recv.at[u], {"ctx": sibling})
+    def grad_copy(u, low):
+        return remote(
+            grads.at[pl.ds(low, 2), theirs + u], gother.at[pl.ds(low - 1, 2), u],
+            g_send.at[low // 2, u], g_recv.at[low // 2, u], {"ctx": sibling},
+        )
 
     def grad0_copy():
-        return remote(grads.at[0], g0other, g_send.at[half], g_recv.at[half], {"ctx": sibling})
+        return remote(grads.at[0], g0other, g_send.at[2, 0], g_recv.at[2, 0], {"ctx": sibling})
 
     def start_tree(u):
         state_copy(u, mine).wait_recv()
@@ -178,7 +199,7 @@
         tree_copy(0, u).start()
 
     def start_dtree(u):
-        grad_copy(u).wait_recv()
+        grad_copy(u, 3).wait_recv()
         dsend[3, u] = grads[4, mine + u] + gother[3, u]
         dtree_copy(3, u).start()
 
@@ -206,6 +227,10 @@
         @pl.when(level > 0)
         def _():
             dtree[mine + u] = dtree[mine + u] + drecv[back, u]
+
+        @pl.when(level == 1)
+        def _():
+            grad_copy(u, 1).wait_recv()
 
         @pl.when(level < 3)
         def _():
@@ -242,9 +267,14 @@
     fill_lambda(hot, table_ref, wide, diag, factor)
 
     def grad_step(u, carry):
-        make_grad(theirs + u)
-        grad_copy(u).start()
-        make_grad(mine + u)
+        load(2, theirs + u).wait()
+        load(3, theirs + u).wait()
+        make_grad(theirs + u, 0, 5)
+        grad_copy(u, 3).start()
+        grad_copy(u, 1).start()
+        load(2, mine + u).wait()
+        load(3, mine + u).wait()
+        make_grad(mine + u, 0, 5)
 
         @pl.when(u >= 1)
         def _():
@@ -257,27 +287,29 @@
     grad0_copy().start()
     start_dtree(3)
 
-    def local_head(h, between):
-        def tile(c):
-            rows = pl.ds(c * SUB, SUB)
-            return rows, qb[h, rows], kb[h, rows], vb[h, rows], gb[h, rows]
-
-        near_grad = {}
-        pair_grad = None
-        for c in range(tiles - 1, -1, -1):
-            if c == 1:
-                between()
-            rows, q, k, v, grad = tile(c)
+    def tile_of(h, c):
+        rows = pl.ds(c * SUB, SUB)
+        return rows, qb[h, rows], kb[h, rows], vb[h, rows], gb[h, rows]
+
+    def score_head(h, weighted, dscore):
+        for c in range(tiles):
+            rows, q, k, v, grad = tile_of(h, c)
             score = mm(q, k, NT)
             back = mm(grad, v, NT)
             wsum[c] += score * back
             weight = diag[c]
-            weighted = (weight * score).astype(BF16)
-            dscore = (weight * back).astype(BF16)
-            out = mm(weighted, v, NN)
-            qg = mm(dscore, k, NN)
-            kg = mm(dscore, q, TN)
-            vg = mm(weighted, grad, TN)
+            weighted[c] = (weight * score).astype(BF16)
+            dscore[c] = (weight * back).astype(BF16)
+
+    def local_head(h, weighted, dscore):
+        near_grad = {}
+        pair_grad = None
+        for c in range(tiles - 1, -1, -1):
+            rows, q, k, v, grad = tile_of(h, c)
+            out = mm(weighted[c], v, NN)
+            qg = mm(dscore[c], k, NN)
+            kg = mm(dscore[c], q, TN)
+            vg = mm(weighted[c], grad, TN)
             use = ([0] if c % 2 else []) + ([1] if c >= 2 else [])
             if use:
                 buckets = ([near[h, c // 2]] if c % 2 else []) + ([near[h, 2]] if c >= 2 else [])
@@ -304,93 +336,97 @@
             if c < 2:
                 dstate = pair_grad if dstate is None else dstate + pair_grad
             if dstate is not None:
-                dlocal[c] = dstate
+                part[h, c] = dstate
             lout[h, rows] = out
             lq[h, rows] = qg
             lk[h, rows] = kg
             lv[h, rows] = vg
-        return dlocal
-
-    dlocal = {}
-
-    def local_step(h, carry):
-        def comm_step(step):
-            @pl.when((step >= TREE_LAG) & (step < TREE_LAG + 3 * half))
-            def _():
-                tree_step(step - TREE_LAG + half)
-
-            @pl.when(step >= half)
-            def _():
-                dtree_step(step - half)
-
-        local_head(h, lambda: comm_step(2 * h))
-        for c in range(3):
-            part[h, c] = dlocal[c]
+
+    def comm_step(step):
+        @pl.when((step >= TREE_LAG) & (step < TREE_LAG + 3 * half))
+        def _():
+            tree_step(step - TREE_LAG + half)
+
+        @pl.when(step >= DTREE_LAG)
+        def _():
+            dtree_step(step - DTREE_LAG)
+
+    def local_step(i, carry):
+        h = 2 * i
+        local_head(h, pa, da)
+        score_head(h + 1, pb, db)
+        comm_step(2 * h)
         comm_step(2 * h + 1)
+        local_head(h + 1, pb, db)
+        score_head(h + 2, pa, da)
+        comm_step(2 * h + 2)
+        comm_step(2 * h + 3)
         return carry
 
-    lax.fori_loop(0, heads, local_step, 0)
+    score_head(0, pa, da)
+    lax.fori_loop(0, heads // 2 - 1, local_step, 0)
+    local_head(heads - 2, pa, da)
+    score_head(heads - 1, pb, db)
+    comm_step(2 * heads - 4)
+    comm_step(2 * heads - 3)
+    local_head(heads - 1, pb, db)
+    comm_step(2 * heads - 2)
+    comm_step(2 * heads - 1)
 
     lane = lax.broadcasted_iota(jnp.int32, (table_ref.shape[1], 128), 1)
     hot = one_hot(index_ref[...], table_ref.shape[1])
-    rows_id = lax.broadcasted_iota(jnp.int32, (SUB, SUB), 0)
-    cols_id = lax.broadcasted_iota(jnp.int32, (SUB, SUB), 1)
+    rows_id = lax.broadcasted_iota(jnp.int32, (128, 128), 0)
+    cols_id = lax.broadcasted_iota(jnp.int32, (128, 128), 1)
     crossed = jnp.bitwise_xor(rows_id, cols_id)
     table = jnp.zeros(lane.shape, F32)
-    for level in range(11):
-        if level < 9:
-            low = (1 << (level - 1)) if level else 0
-            mask = (crossed >= low) & (crossed < (1 << level)) & (cols_id <= rows_id)
-            values = []
-            for c in range(tiles):
-                value = jnp.where(mask, wsum[c], 0.0)
-                values.append(value[:, :128] + value[:, 128:])
-            value = jnp.concatenate(values, axis=0)
-        else:
-            value = lsum[level - 9]
-        table = jnp.where(lane == level, row_sums(hot, value), table)
+    blocks = [wsum[n // 2, (n % 2) * 128 : (n % 2 + 1) * 128, (n % 2) * 128 : (n % 2 + 1) * 128] for n in range(2 * tiles)]
+    high, rest, _ = split3(jnp.concatenate(blocks, axis=0))
+    for level in range(8):
+        low = (1 << (level - 1)) if level else 0
+        mask = (crossed >= low) & (crossed < (1 << level)) & (cols_id <= rows_id)
+        mask = jnp.where(mask, 1.0, 0.0).astype(BF16)
+        mask = jnp.concatenate([mask] * (2 * tiles), axis=0)
+        total = mm(hot, high * mask, NN) + mm(hot, rest * mask, NN)
+        table = jnp.where(lane == level, jnp.sum(total, axis=1, keepdims=True), table)
+    lower = [wsum[c, 128:256, 0:128] for c in range(tiles)]
+    clear = jnp.zeros((128, 128), F32)
+    lower = jnp.concatenate([piece for block in lower for piece in (clear, block)], axis=0)
+    table = jnp.where(lane == 8, row_sums(hot, lower), table)
+    for level in range(9, 11):
+        table = jnp.where(lane == level, row_sums(hot, lsum[level - 9]), table)
 
     rest_copy(theirs).wait_recv()
     for level in range(4):
         for u in range(half):
             relay(level, u, theirs).wait_recv()
 
-    def cross_step(h, carry):
-        cat[h, :, 0:128] = jnp.where(bits[0], sother[h], 0.0).astype(BF16)
+    def lam_step(h, carry):
+        buckets = [jnp.where(bits[0], sother[h], 0.0).astype(BF16)]
         for j in range(1, 5):
-            cat[h, :, j * 128 : (j + 1) * 128] = jnp.where(bits[j], recv[j - 1, h], 0.0).astype(BF16)
-        joined = cat[h]
+            buckets.append(jnp.where(bits[j], recv[j - 1, h], 0.0).astype(BF16))
+        stack[h] = jnp.concatenate(buckets, axis=0)
+        joined = jnp.concatenate(buckets, axis=1)
         for c in range(tiles):
             rows = pl.ds(c * SUB, SUB)
             cross = mm(qb[h, rows], joined, NN)
             wide_grad = gb[h, rows].astype(F32)
-            out = lout[h, rows]
             for j in range(5):
-                piece = cross[:, j * 128 : (j + 1) * 128]
-                out += wide[2 + j, rows] * piece
-                lsum[2 + j, rows] += piece * wide_grad
-            out_ref[h, rows] = out.astype(BF16)
-
-        @pl.when(h % 2 == 1)
-        def _():
-            dtree_step(3 * half + h // 2)
-
+                lsum[2 + j, rows] += cross[:, j * 128 : (j + 1) * 128] * wide_grad
         return carry
 
-    lax.fori_loop(0, heads, cross_step, 0)
+    lax.fori_loop(0, heads, lam_step, 0)
     for level in range(11, 16):
         table = jnp.where(lane == level, row_sums(hot, lsum[level - 9]), table)
 
-    spots = (z * 2 + core, y, x)
-    sizes = (8, 4, 4)
+    spots = (z * 2 + core, x * 4 + y)
+    sizes = (8, 16)
     psum[0, spots[0]] = (table * scale).T[0:16]
 
     def table_copy(phase, d):
         other = (spots[phase] + d) % sizes[phase]
         device = (
-            {"ctx": at(x, y) - core + other % 2, "heads": other // 2},
-            {"ctx": at(x, other)},
-            {"ctx": at(other, y)},
+            {"ctx": me - core + other % 2, "heads": other // 2},
+            {"ctx": at(other // 4, other % 4)},
         )[phase]
         slot = psum.at[phase, spots[phase]]
         return remote(slot, slot, p_send.at[phase, d - 1], p_recv.at[phase, d - 1], device)
@@ -409,25 +445,44 @@
         value = psum[phase, 0]
         for n in range(1, sizes[phase]):
             value = value + psum[phase, n]
-        if phase < 2:
-            psum[phase + 1, spots[phase + 1]] = value
-            for d in range(1, 4):
-                table_copy(phase + 1, d).start()
+        if phase < 1:
+            psum[1, spots[1]] = value
+            for d in range(1, 16):
+                table_copy(1, d).start()
         else:
             total_ref[...] = value[:, 0:64]
 
+    def out_step(h, carry):
+        joined = jnp.concatenate([stack[h, j * 128 : (j + 1) * 128] for j in range(5)], axis=1)
+        for c in range(tiles):
+            rows = pl.ds(c * SUB, SUB)
+            cross = mm(qb[h, rows], joined, NN)
+            out = lout[h, rows]
+            for j in range(5):
+                out += wide[2 + j, rows] * cross[:, j * 128 : (j + 1) * 128]
+            out_ref[h, rows] = out.astype(BF16)
+
+        @pl.when(h < DTREE_LAG)
+        def _():
+            dtree_step(4 * half - DTREE_LAG + h)
+
+        return carry
+
+    lax.fori_loop(0, heads, out_step, 0)
+    table_phase(0)
     for u in range(half):
         dtree_relay(u, theirs).wait_recv()
     grad0_copy().wait_recv()
 
     def grad_head(h):
-        joined = cat[h]
+        joined = stack[h]
         far = dtree[h] + jnp.where(bits[0], 0.0, g0other[h])
         for c in range(tiles):
             rows = pl.ds(c * SUB, SUB)
-            wide_grad = gb[h, rows].astype(F32)
-            scaled = jnp.concatenate([(wide[2 + j, rows] * wide_grad).astype(BF16) for j in range(5)], axis=1)
-            qg = lq[h, rows] + mm(scaled, joined, NT)
+            back = mm(gb[h, rows], joined, NT)
+            qg = lq[h, rows]
+            for j in range(5):
+                qg += wide[2 + j, rows] * back[:, j * 128 : (j + 1) * 128]
             dstate = (far + part[h, c] if c < 3 else far).astype(BF16)
             kg = lk[h, rows] + mm(vb[h, rows], dstate, NT)
             vg = lv[h, rows] + mm(kb[h, rows], dstate, NN)
@@ -442,24 +497,21 @@
 
         lax.fori_loop(low, high, step, 0)
 
-    grad_loop(0, 3)
-    table_phase(0)
-    grad_loop(3, 6)
+    grad_loop(0, heads)
     table_phase(1)
-    grad_loop(6, heads)
-    table_phase(2)
 
     rest_copy(mine).wait_send()
     grad0_copy().wait_send()
     for u in range(half):
         state_copy(u, theirs).wait_send()
-        grad_copy(u).wait_send()
+        grad_copy(u, 1).wait_send()
+        grad_copy(u, 3).wait_send()
         for level in range(4):
             tree_copy(level, u).wait_send()
             relay(level, u, mine).wait_send()
             dtree_copy(level, u).wait_send()
         dtree_relay(u, mine).wait_send()
-    for phase in range(3):
+    for phase in range(2):
         for d in range(1, sizes[phase]):
             table_copy(phase, d).wait_send()
 
@@ -504,7 +556,11 @@
             pltpu.VMEM((7, length, 128), F32),
             pltpu.VMEM((heads, 3) + square, BF16),
             pltpu.VMEM((heads, 3) + square, F32),
-            pltpu.VMEM((heads, width, 5 * width), BF16),
+            pltpu.VMEM((heads, 5 * width, width), BF16),
+            pltpu.VMEM((tiles, SUB, SUB), BF16),
+            pltpu.VMEM((tiles, SUB, SUB), BF16),
+            pltpu.VMEM((tiles, SUB, SUB), BF16),
+            pltpu.VMEM((tiles, SUB, SUB), BF16),
             pltpu.VMEM((heads,) + square, F32),
             pltpu.VMEM((heads,) + square, F32),
             pltpu.VMEM((5, heads) + square, F32),
@@ -515,13 +571,13 @@
             pltpu.VMEM((4, half) + square, F32),
             pltpu.VMEM((4, half) + square, F32),
             pltpu.VMEM((heads,) + square, F32),
-            pltpu.VMEM((3, 8, 16, table_lanes), F32),
-            dma(4, heads), dma(half + 1), dma(half + 1), dma(half + 1), dma(half + 1),
+            pltpu.VMEM((2, 16, 16, table_lanes), F32),
+            dma(4, heads), dma(half + 1), dma(half + 1), dma(3, half), dma(3, half),
             dma(4, half), dma(4, half), dma(4, half), dma(4, half),
-            dma(4, half), dma(4, half), dma(half), dma(half), dma(3, 7), dma(3, 7),
+            dma(4, half), dma(4, half), dma(half), dma(half), dma(2, 15), dma(2, 15),
         ],
         compiler_params=pltpu.CompilerParams(
-            collective_id=0, has_side_effects=True, vmem_limit_bytes=52 << 20
+            collective_id=0, has_side_effects=True, vmem_limit_bytes=54 << 20
         ),
     )(queries, keys, values, out_grad, table_index.reshape(1, length), level_table.T)
     outs = pl.pallas_call(

time: 61.6 us -> 58.5 us (0.950); the launches traced: 60.7 us -> 58.3 us
  Pallas kernels: 60.1 us -> 57.6 us
    pallas_call x1, Pallas kernels: 56.6 us -> 54.2 us  [body(): pl.pallas_call(functools.partial(kernel, factor=factor, scale=factor / ma...]
where the time goes in v4:
time: 58.5 us; the launch traced here: 58.3 us
  Pallas kernels  57.6 us (98%)
  between operations  0.64 us (1%)
    pallas_call x1, Pallas kernels, body(): pl.pallas_call(functools.partial(kernel, factor=factor, scale=factor / ma...  54.2 us
    pallas_call x1, Pallas kernels, body(): pl.pallas_call(put_kernel, out_shape=tuple((jax.ShapeDtypeStruct(queries....  3.43 us

profile of v4, /device:TPU:1, one launch (start us, length us, event | category | flops | bytes accessed | tf_op | source)
XLA Modules:
  0.0 58.3 jit_solution(892238678947420596)
XLA Ops:
  0.6 54.2 %shard_map.101 = (bf16[8,1024,128]{2,1,0:T(8,128)(2,1)S(1)}, bf16[8,1024,128]{2,1,0:T(8,128)(2,1)S(1)}, bf16[8,1024,128]{2,1,0:T(8,128)(2,1)S(1)}, bf16[8,1024,128]{2,1,0:T(8,128)(2,1)S(1)}, f32[16,64]{1,0:T(8,128)S(1)}) custom-call(bf16[8,1024,128]{2,1,0:T(8,128)(2,1)} %q_hbm.1, bf16[8,1024,128]{2,1,0:T(8,128)(2,1)} %k_hbm.1, bf16[8,1024,128]{2,1,0:T(8,128)(2,1)} %v_hbm.1, ...), custom_call_target="tpu_custom_call" | custom-call | tf_op jit(solution)/shard_map/pallas_call | solution.py:544
  54.9 3.4 %shard_map.102 = (bf16[8,1024,128]{2,1,0:T(8,128)(2,1)}, bf16[8,1024,128]{2,1,0:T(8,128)(2,1)}, bf16[8,1024,128]{2,1,0:T(8,128)(2,1)}, bf16[8,1024,128]{2,1,0:T(8,128)(2,1)}, f32[16,64]{1,0:T(8,128)}) custom-call(bf16[8,1024,128]{2,1,0:T(8,128)(2,1)S(1)} %get-tuple-element.15.refs_0_, bf16[8,1024,128]{2,1,0:T(8,128)(2,1)S(1)} %get-tuple-element.16.refs_1_, ...), custom_call_target="tpu_custom_call" | custom-call | tf_op jit(solution)/shard_map/pallas_call | solution.py:583

commit v5 on v4

--- a/solution.py
+++ b/solution.py
@@ -10,7 +10,7 @@
 
 SUB = 256
 PARTNERS = 22
-TREE_LAG = 1
+TREE_LAG = 0
 DTREE_LAG = 4
 MESH = pl.DeviceIdType.MESH
 F32 = jnp.float32
@@ -294,22 +294,32 @@
     def score_head(h, weighted, dscore):
         for c in range(tiles):
             rows, q, k, v, grad = tile_of(h, c)
-            score = mm(q, k, NT)
-            back = mm(grad, v, NT)
-            wsum[c] += score * back
-            weight = diag[c]
-            weighted[c] = (weight * score).astype(BF16)
-            dscore[c] = (weight * back).astype(BF16)
+            for part_rows, count in ((slice(0, 128), 128), (slice(128, 256), 256)):
+                score = mm(q[part_rows], k[:count], NT)
+                back = mm(grad[part_rows], v[:count], NT)
+                spot = pl.ds(part_rows.start, 128)
+                wsum[c, spot, 0:count] += score * back
+                weight = diag[c, spot, 0:count]
+                weighted[c, spot, 0:count] = (weight * score).astype(BF16)
+                dscore[c, spot, 0:count] = (weight * back).astype(BF16)
 
     def local_head(h, weighted, dscore):
         near_grad = {}
         pair_grad = None
         for c in range(tiles - 1, -1, -1):
             rows, q, k, v, grad = tile_of(h, c)
-            out = mm(weighted[c], v, NN)
-            qg = mm(dscore[c], k, NN)
-            kg = mm(dscore[c], q, TN)
-            vg = mm(weighted[c], grad, TN)
+            def lower(score, right):
+                upper = mm(score[c, 0:128, 0:128], right[:128], NN)
+                return jnp.concatenate([upper, mm(score[c, 128:256], right, NN)], axis=0)
+
+            def lower_t(score, right):
+                upper = mm(score[c, :, 0:128], right, TN)
+                return jnp.concatenate([upper, mm(score[c, 128:256, 128:256], right[128:], TN)], axis=0)
+
+            out = lower(weighted, v)
+            qg = lower(dscore, k)
+            kg = lower_t(dscore, q)
+            vg = lower_t(weighted, grad)
             use = ([0] if c % 2 else []) + ([1] if c >= 2 else [])
             if use:
                 buckets = ([near[h, c // 2]] if c % 2 else []) + ([near[h, 2]] if c >= 2 else [])

time: 58.5 us -> 58.3 us (level)
  no operation moved by 1% of the time
where the time goes in v5:
time: 58.3 us; the launch traced here: 58.2 us
  Pallas kernels  57.5 us (99%)
  between operations  0.64 us (1%)
    pallas_call x1, Pallas kernels, body(): pl.pallas_call(functools.partial(kernel, factor=factor, scale=factor / ma...  54.1 us
    pallas_call x1, Pallas kernels, body(): pl.pallas_call(put_kernel, out_shape=tuple((jax.ShapeDtypeStruct(queries....  3.43 us

profile of v5, /device:TPU:1, one launch (start us, length us, event | category | flops | bytes accessed | tf_op | source)
XLA Modules:
  0.0 58.2 jit_solution(17548928123448875250)
XLA Ops:
  0.6 54.1 %shard_map.101 = (bf16[8,1024,128]{2,1,0:T(8,128)(2,1)S(1)}, bf16[8,1024,128]{2,1,0:T(8,128)(2,1)S(1)}, bf16[8,1024,128]{2,1,0:T(8,128)(2,1)S(1)}, bf16[8,1024,128]{2,1,0:T(8,128)(2,1)S(1)}, f32[16,64]{1,0:T(8,128)S(1)}) custom-call(bf16[8,1024,128]{2,1,0:T(8,128)(2,1)} %q_hbm.1, bf16[8,1024,128]{2,1,0:T(8,128)(2,1)} %k_hbm.1, bf16[8,1024,128]{2,1,0:T(8,128)(2,1)} %v_hbm.1, ...), custom_call_target="tpu_custom_call" | custom-call | tf_op jit(solution)/shard_map/pallas_call | solution.py:554
  54.7 3.4 %shard_map.102 = (bf16[8,1024,128]{2,1,0:T(8,128)(2,1)}, bf16[8,1024,128]{2,1,0:T(8,128)(2,1)}, bf16[8,1024,128]{2,1,0:T(8,128)(2,1)}, bf16[8,1024,128]{2,1,0:T(8,128)(2,1)}, f32[16,64]{1,0:T(8,128)}) custom-call(bf16[8,1024,128]{2,1,0:T(8,128)(2,1)S(1)} %get-tuple-element.15.refs_0_, bf16[8,1024,128]{2,1,0:T(8,128)(2,1)S(1)} %get-tuple-element.16.refs_1_, ...), custom_call_target="tpu_custom_call" | custom-call | tf_op jit(solution)/shard_map/pallas_call | solution.py:593
